TPU v7x, 512 devices: a whole 4x4x16 slice. The times are simulated.
512 devices in a mesh: dom: 64 (over z_hi, x, y, core), grp: 8 (over z_lo).
Axes of the slice: x: 4, y: 4, z: 16 (z_hi: 2, z_lo: 8; z = z_hi * 8 + z_lo), core: 2. Of those that a mesh axis runs over, the one named last changes fastest.
Arguments:
- features: bfloat16 [4096, 768], P(('dom', 'grp')), may hold values from -6 to 6
- w_first: bfloat16 [768, 512], replicated, may hold values from -0.21875 to 0.21875
- w_second: bfloat16 [512, 512], replicated, may hold values from -0.25 to 0.25
- relation_table: bfloat16 [1387, 512], replicated, may hold values from -1.5 to 1.5
- heads: int32 [2, 65536], P(None, ('dom', 'grp')), may hold values from 0 to 63
- relations: int32 [2, 65536], P(None, ('dom', 'grp')), may hold values from 0 to 1386
- tails: int32 [2, 65536], P(None, ('dom', 'grp')), may hold values from 0 to 63
- negatives: int32 [2, 512], replicated, may hold values from 0 to 63
- partner: int32 [2, 64], replicated, may hold values from 0 to 63, as said below
Outputs:
- edge_loss: float32 [2, 65536], P(None, ('dom', 'grp'))
- grad_w1: float32 [768, 512], P('grp')
- grad_w2: float32 [512, 512], P('grp')
Inputs may be any that keep to these rules, and one draw needn't show every extreme that they name: partner[r, p] = p XOR m_r with one mask m_r of 1 to 63 for each round r, so partitions meet in pairs.
All inputs are finite; a program needn't handle non-finite values.
Results may differ from a plain program's by a relative error of at most 0.0095.
Values may be sent and summed in bfloat16 or wider, within the bound.
A program may use at most 64 MiB of HBM per device.

v0:
```python
import math

import jax
import jax.numpy as jnp
from jax import lax
from jax.sharding import PartitionSpec as P


def in_order(pieces, dim):
    pieces = jnp.moveaxis(pieces, 0, dim)
    dims = pieces.shape
    return pieces.reshape(*dims[:dim], dims[dim] * dims[dim + 1], *dims[dim + 2 :])


def from_everyone(value, axis):
    copies = jnp.broadcast_to(value, (lax.axis_size(axis), *value.shape))
    return lax.all_to_all(copies, axis, split_axis=0, concat_axis=0, tiled=True)


def collect(value, axis, dim):
    return in_order(from_everyone(value, axis), dim)


def partner_2(value, axis, distance):
    return lax.ppermute(value, axis, [(i, i ^ 1 << distance) for i in range(lax.axis_size(axis))])


def in_blocks(value, dim, length):
    before, after = (value.shape[:dim], value.shape[dim + 1 :])
    return jnp.moveaxis(value.reshape(*before, length, -1, *after), dim, 0)


def summed_on_arrival(value, axis, dim):
    length = lax.axis_size(axis)
    pieces = lax.all_to_all(in_blocks(value, dim, length), axis, 0, 0, tiled=True)
    return jnp.sum(pieces.astype(jnp.float32), axis=0)


def encode(rows, w_first, w_second):
    pre_act = jnp.dot(rows, w_first, preferred_element_type=jnp.float32)
    hidden = jax.nn.silu(pre_act).astype(jnp.bfloat16)
    encoded = jnp.dot(hidden, w_second, preferred_element_type=jnp.float32).astype(jnp.bfloat16)
    return (pre_act, hidden, encoded)


def backward(rows, pre_act, hidden, grad_rows, w_second):
    term_second = lax.dot_general(
        hidden, grad_rows, (((0,), (0,)), ((), ())), preferred_element_type=jnp.float32
    )
    grad_hidden = lax.dot_general(
        grad_rows, w_second, (((1,), (1,)), ((), ())), preferred_element_type=jnp.float32
    )
    sigmoid_pre = jax.nn.sigmoid(pre_act)
    silu_slope = sigmoid_pre * (1.0 + pre_act * (1.0 - sigmoid_pre))
    grad_pre = (grad_hidden * silu_slope).astype(jnp.bfloat16)
    term_first = lax.dot_general(
        rows, grad_pre, (((0,), (0,)), ((), ())), preferred_element_type=jnp.float32
    )
    return (term_first, term_second)


def row_select(ids, row_count):
    return ids[:, None] == jnp.arange(row_count, dtype=jnp.int32)[None, :]


def pick_rows(selector, table):
    return jnp.dot(selector.astype(jnp.bfloat16), table, preferred_element_type=jnp.float32)


def add_into_rows(selector, values):
    return lax.dot_general(
        selector.astype(jnp.float32),
        values,
        (((0,), (0,)), ((), ())),
        precision=lax.Precision.HIGHEST,
        preferred_element_type=jnp.float32,
    )


def score_block(own, other, relation_table, head_ids, relation_ids, tail_ids, negative_ids):
    half_width = own.shape[1] // 2
    row_count = own.shape[0]
    head_select = row_select(head_ids, row_count)
    tail_select = row_select(tail_ids, row_count)
    negative_select = row_select(negative_ids, row_count)
    head_rows = pick_rows(head_select, own)
    rel_rows = jnp.take(relation_table, relation_ids, axis=0).astype(jnp.float32)
    tail_rows = pick_rows(tail_select, other)
    negative_rows = pick_rows(negative_select, other).astype(jnp.bfloat16)
    head_real, head_imag = (head_rows[:, :half_width], head_rows[:, half_width:])
    rel_real, rel_imag = (rel_rows[:, :half_width], rel_rows[:, half_width:])
    query = jnp.concatenate(
        [head_real * rel_real - head_imag * rel_imag, head_real * rel_imag + head_imag * rel_real],
        axis=1,
    ).astype(jnp.bfloat16)
    query_wide = query.astype(jnp.float32)
    positive = jnp.sum(query_wide * tail_rows, axis=1)
    negative = lax.dot_general(
        query, negative_rows, (((1,), (1,)), ((), ())), preferred_element_type=jnp.float32
    )
    edge_loss = (
        jax.nn.softplus(-positive) + jnp.sum(jax.nn.softplus(negative), axis=1) / negative.shape[1]
    )
    weight_neg = (jax.nn.sigmoid(negative) / negative.shape[1]).astype(jnp.bfloat16)
    weight_pos = -jax.nn.sigmoid(-positive)
    grad_query = weight_pos[:, None] * tail_rows + jnp.dot(
        weight_neg, negative_rows, preferred_element_type=jnp.float32
    )
    grad_tail = weight_pos[:, None] * query_wide
    grad_negative = lax.dot_general(
        weight_neg, query, (((0,), (0,)), ((), ())), preferred_element_type=jnp.float32
    )
    grad_real, grad_imag = (grad_query[:, :half_width], grad_query[:, half_width:])
    grad_head = jnp.concatenate(
        [grad_real * rel_real + grad_imag * rel_imag, grad_imag * rel_real - grad_real * rel_imag],
        axis=1,
    )
    own_part = add_into_rows(head_select, grad_head)
    far_part = add_into_rows(tail_select, grad_tail) + add_into_rows(negative_select, grad_negative)
    return (edge_loss, own_part, far_part)


def route_rows(payload, xor_mask, bit_count, mover):
    for bit_level in range(bit_count):
        swapped = mover(payload, bit_level)
        payload = jnp.where(xor_mask >> bit_level & 1 == 1, swapped, payload)
    return payload


def per_device(
    features, w_first, w_second, relation_table, heads, relations, tails, negatives, partner
):
    pre_act, hidden, encoded = encode(features, w_first, w_second)
    own_block = collect(encoded, "grp", 0)
    bit_count = lax.axis_size("dom").bit_length() - 1
    total_first = jnp.zeros(w_first.shape, jnp.float32)
    total_second = jnp.zeros(w_second.shape, jnp.float32)
    own_acc = jnp.zeros(own_block.shape, jnp.float32)
    losses = []
    for bucket in range(heads.shape[0]):
        xor_mask = partner[bucket, 0]
        far_features = route_rows(
            features,
            xor_mask,
            bit_count,
            lambda payload, bit_level: partner_2(payload, "dom", bit_level),
        )
        far_pre, far_hidden, arrived = encode(far_features, w_first, w_second)
        far_block = collect(arrived, "grp", 0)
        edge_loss, own_part, far_part = score_block(
            own_block,
            far_block,
            relation_table,
            heads[bucket],
            relations[bucket],
            tails[bucket],
            negatives[bucket],
        )
        losses.append(edge_loss)
        own_acc = own_acc + own_part
        far_grad = summed_on_arrival(far_part.astype(jnp.bfloat16), "grp", 0).astype(jnp.bfloat16)
        term_first, term_second = backward(far_features, far_pre, far_hidden, far_grad, w_second)
        total_first = total_first + term_first
        total_second = total_second + term_second
    own_grad = summed_on_arrival(own_acc.astype(jnp.bfloat16), "grp", 0).astype(jnp.bfloat16)
    term_first, term_second = backward(features, pre_act, hidden, own_grad, w_second)
    total_first = total_first + term_first
    total_second = total_second + term_second
    group_size = lax.axis_size("grp")
    summed_first, summed_second = lax.psum((total_first, total_second), ("dom", "grp"))
    squares = jnp.sum(summed_first * summed_first) + jnp.sum(summed_second * summed_second)
    share_first = summed_first.shape[0] // group_size
    share_second = summed_second.shape[0] // group_size
    position = lax.axis_index("grp")
    summed_first = lax.dynamic_slice_in_dim(summed_first, position * share_first, share_first, 0)
    summed_second = lax.dynamic_slice_in_dim(
        summed_second, position * share_second, share_second, 0
    )
    factor = jnp.minimum(1.0, math.sqrt(w_first.size + w_second.size) / jnp.sqrt(squares + 1e-06))
    return (jnp.stack(losses), summed_first * factor, summed_second * factor)


def solution(mesh):
    return jax.shard_map(
        per_device,
        mesh=mesh,
        in_specs=(
            P(("dom", "grp"), None),
            P(),
            P(),
            P(),
            P(None, ("dom", "grp")),
            P(None, ("dom", "grp")),
            P(None, ("dom", "grp")),
            P(),
            P(),
        ),
        out_specs=(P(None, ("dom", "grp")), P("grp", None), P("grp", None)),
        check_vma=False,
    )
```

profile of v0, /device:TPU:1, one launch (start us, length us, event | category | flops | bytes accessed | tf_op | source)
XLA Modules:
  0.0 680.0 jit_solution(16580233287284113734)
XLA Ops:
  7.2 8.9 %collective-permute-start = (bf16[8,768]{1,0:T(8,128)(2,1)}, bf16[8,768]{1,0:T(8,128)(2,1)S(1)}, u32[]{:S(2)}, u32[]{:S(2)}) collective-permute-start(bf16[8,768]{1,0:T(8,128)(2,1)} %param.11), channel_id=1, source_target_pairs={{0,8},{8,0},{16,24},{24,16},{32,40},{40,32},{48,56},{56,48},{64,72... | collective-permute-start | bytes 36872 | tf_op jit(solution)/shard_map/ppermute | solution.py:25
  19.3 6.9 %all-to-all-start = ((bf16[8,8,512]{2,1,0:T(8,128)(2,1)}), bf16[8,8,512]{2,1,0:T(8,128)(2,1)S(1)}, u32[]{:S(2)}, u32[]{:S(2)}) async-start(bf16[8,8,512]{2,1,0:T(8,128)(2,1)} %broadcast_in_dim.15), calls=%async_computation | async-start | bytes 131072 | tf_op jit(solution)/shard_map/all_to_all | solution.py:17
  32.0 3.2 collective-permute-start.6
  44.3 4.8 collective-permute-start.7
  51.2 3.1 collective-permute-start.8
  55.1 3.1 collective-permute-start.3
  58.3 4.4 collective-permute-start.9
  65.2 7.9 %collective-permute-start.10 = (bf16[8,768]{1,0:T(8,128)(2,1)S(1)}, bf16[8,768]{1,0:T(8,128)(2,1)S(1)}, u32[]{:S(2)}, u32[]{:S(2)}) collective-permute-start(bf16[8,768]{1,0:T(8,128)(2,1)S(1)} %broadcast_select_fusion.4), channel_id=1, source_target_pairs={{0,256},{8,264},{16,272},{24,280},{32,288},{40,296},{48,304},{56,3... | collective-permute-start | bytes 36872 | tf_op jit(solution)/shard_map/ppermute | solution.py:25
  73.1 6.1 collective-permute-start.5
  79.6 6.7 collective-permute-done.5
  87.3 9.3 %all-to-all-start.1 = ((bf16[8,8,512]{2,1,0:T(8,128)(2,1)}), bf16[8,8,512]{2,1,0:T(8,128)(2,1)S(1)}, u32[]{:S(2)}, u32[]{:S(2)}) async-start(bf16[8,8,512]{2,1,0:T(8,128)(2,1)} %broadcast_in_dim.16), calls=%async_computation.1 | async-start | bytes 131072 | tf_op jit(solution)/shard_map/all_to_all | solution.py:17
  98.0 8.5 %all-to-all-done.1 = bf16[8,8,512]{2,1,0:T(8,128)(2,1)S(1)} async-done(((bf16[8,8,512]{2,1,0:T(8,128)(2,1)}), bf16[8,8,512]{2,1,0:T(8,128)(2,1)S(1)}, u32[]{:S(2)}, u32[]{:S(2)}) %all-to-all-start.1) | async-done | bytes 65568 | tf_op jit(solution)/shard_map/all_to_all | solution.py:17
  107.0 4.0 all-to-all-start.2
  116.5 4.3 all-to-all-done.2
  129.7 5.0 all-to-all-start.5
  134.7 2.4 fusion.3
  139.0 5.4 all-to-all-done.5
  144.4 3.9 all-to-all-start.3
  150.1 8.0 %all-to-all-done.3 = bf16[8,8,512]{2,1,0:T(8,128)(2,1)S(1)} async-done(((bf16[8,8,512]{2,1,0:T(8,128)(2,1)}), bf16[8,8,512]{2,1,0:T(8,128)(2,1)S(1)}, u32[]{:S(2)}, u32[]{:S(2)}) %all-to-all-start.3) | async-done | bytes 65568 | tf_op jit(solution)/shard_map/all_to_all | solution.py:35
  158.1 3.4 all-to-all-start.4
  161.9 9.3 %all-to-all-done.4 = bf16[8,8,512]{2,1,0:T(8,128)(2,1)S(1)} async-done(((bf16[8,8,512]{2,1,0:T(8,128)(2,1)}), bf16[8,8,512]{2,1,0:T(8,128)(2,1)S(1)}, u32[]{:S(2)}, u32[]{:S(2)}) %all-to-all-start.4) | async-done | bytes 65568 | tf_op jit(solution)/shard_map/all_to_all | solution.py:35
  174.5 3.2 bitcast_add_fusion
  179.0 487.2 %all-reduce.3.cloned.1.call-done = (f32[768,512]{1,0:T(8,128)}, f32[512,512]{1,0:T(8,128)}) async-done(((f32[768,512]{1,0:T(8,128)}, f32[512,512]{1,0:T(8,128)}), (f32[768,512]{1,0:T(8,128)}, f32[512,512]{1,0:T(8,128)})) %all-reduce.3.cloned.1.call-update) | async-done | bytes 2621456 | tf_op jit(solution)/shard_map/psum | solution.py:170
  666.2 2.5 multiply_reduce_fusion
  (165 shorter events, 44.8 us)
Async XLA Ops:
  7.2 24.8 %collective-permute-start = (bf16[8,768]{1,0:T(8,128)(2,1)}, bf16[8,768]{1,0:T(8,128)(2,1)S(1)}, u32[]{:S(2)}, u32[]{:S(2)}) collective-permute-start(bf16[8,768]{1,0:T(8,128)(2,1)} %param.11), channel_id=1, source_target_pairs={{0,8},{8,0},{16,24},{24,16},{32,40},{40,32},{48,56},{56,48},{64,72... | collective-permute-start | bytes 36872 | tf_op jit(solution)/shard_map/ppermute | solution.py:25
  19.3 67.4 %all-to-all-start = ((bf16[8,8,512]{2,1,0:T(8,128)(2,1)}), bf16[8,8,512]{2,1,0:T(8,128)(2,1)S(1)}, u32[]{:S(2)}, u32[]{:S(2)}) async-start(bf16[8,8,512]{2,1,0:T(8,128)(2,1)} %broadcast_in_dim.15), calls=%async_computation | async-start | bytes 131072 | tf_op jit(solution)/shard_map/all_to_all | solution.py:17
  27.6 83.5 %copy-start.24 = (s32[1,512]{1,0:T(1,128)}, s32[1,512]{1,0:T(1,128)S(1)}, u32[]{:S(2)}) copy-start(s32[1,512]{1,0:T(1,128)S(1)} %get-tuple-element.20) | copy-start | bytes 6148
  28.2 51.0 %copy-start.2 = (bf16[768,512]{1,0:T(8,128)(2,1)S(1)}, bf16[768,512]{1,0:T(8,128)(2,1)}, u32[]{:S(2)}) copy-start(bf16[768,512]{1,0:T(8,128)(2,1)} %param.12) | copy-start | bytes 2359300
  29.1 50.4 %copy-start.1 = (bf16[512,512]{1,0:T(8,128)(2,1)S(1)}, bf16[512,512]{1,0:T(8,128)(2,1)}, u32[]{:S(2)}) copy-start(bf16[512,512]{1,0:T(8,128)(2,1)} %param.13) | copy-start | bytes 1572868
  32.0 12.3 %collective-permute-start.6 = (bf16[8,768]{1,0:T(8,128)(2,1)S(1)}, bf16[8,768]{1,0:T(8,128)(2,1)S(1)}, u32[]{:S(2)}, u32[]{:S(2)}) collective-permute-start(bf16[8,768]{1,0:T(8,128)(2,1)S(1)} %get-tuple-element.19), channel_id=1, source_target_pairs={{0,16},{8,24},{16,0},{24,8},{32,48},{40,56},{48,32},{56,40},{64,80... | collective-permute-start | bytes 36872 | tf_op jit(solution)/shard_map/ppermute | solution.py:25
  35.8 76.7 %copy-start.30 = (s32[128]{0:T(128)}, s32[128]{0:T(128)S(1)}, u32[]{:S(2)}) copy-start(s32[128]{0:T(128)S(1)} %get-tuple-element.22) | copy-start | bytes 1540
  42.2 6.9 %collective-permute-start.1 = (bf16[8,768]{1,0:T(8,128)(2,1)S(1)}, bf16[8,768]{1,0:T(8,128)(2,1)S(1)}, u32[]{:S(2)}, u32[]{:S(2)}) collective-permute-start(bf16[8,768]{1,0:T(8,128)(2,1)S(1)} %get-tuple-element.18), channel_id=1, source_target_pairs={{0,16},{8,24},{16,0},{24,8},{32,48},{40,56},{48,32},{56,40},{64,80... | collective-permute-start | bytes 36872 | tf_op jit(solution)/shard_map/ppermute | solution.py:25
  44.3 6.9 %collective-permute-start.7 = (bf16[8,768]{1,0:T(8,128)(2,1)S(1)}, bf16[8,768]{1,0:T(8,128)(2,1)S(1)}, u32[]{:S(2)}, u32[]{:S(2)}) collective-permute-start(bf16[8,768]{1,0:T(8,128)(2,1)S(1)} %broadcast_select_fusion.1), channel_id=1, source_target_pairs={{0,32},{8,40},{16,48},{24,56},{32,0},{40,8},{48,16},{56,24},{64,96... | collective-permute-start | bytes 36872 | tf_op jit(solution)/shard_map/ppermute | solution.py:25
  49.2 5.9 collective-permute-start.2
  51.2 7.0 %collective-permute-start.8 = (bf16[8,768]{1,0:T(8,128)(2,1)S(1)}, bf16[8,768]{1,0:T(8,128)(2,1)S(1)}, u32[]{:S(2)}, u32[]{:S(2)}) collective-permute-start(bf16[8,768]{1,0:T(8,128)(2,1)S(1)} %broadcast_select_fusion.2), channel_id=1, source_target_pairs={{0,64},{8,72},{16,80},{24,88},{32,96},{40,104},{48,112},{56,120},{... | collective-permute-start | bytes 36872 | tf_op jit(solution)/shard_map/ppermute | solution.py:25
  55.1 41.5 %copy-start.27 = (s32[128]{0:T(128)S(1)}, s32[128]{0:T(128)}, u32[]{:S(2)}) copy-start(s32[128]{0:T(128)} %get-tuple-element.27) | copy-start | bytes 1540
  55.1 7.5 %collective-permute-start.3 = (bf16[8,768]{1,0:T(8,128)(2,1)S(1)}, bf16[8,768]{1,0:T(8,128)(2,1)S(1)}, u32[]{:S(2)}, u32[]{:S(2)}) collective-permute-start(bf16[8,768]{1,0:T(8,128)(2,1)S(1)} %broadcast_select_fusion.8), channel_id=1, source_target_pairs={{0,64},{8,72},{16,80},{24,88},{32,96},{40,104},{48,112},{56,120},{... | collective-permute-start | bytes 36872 | tf_op jit(solution)/shard_map/ppermute | solution.py:25
  58.3 6.8 %collective-permute-start.9 = (bf16[8,768]{1,0:T(8,128)(2,1)S(1)}, bf16[8,768]{1,0:T(8,128)(2,1)S(1)}, u32[]{:S(2)}, u32[]{:S(2)}) collective-permute-start(bf16[8,768]{1,0:T(8,128)(2,1)S(1)} %broadcast_select_fusion.3), channel_id=1, source_target_pairs={{0,128},{8,136},{16,144},{24,152},{32,160},{40,168},{48,176},{56,1... | collective-permute-start | bytes 36872 | tf_op jit(solution)/shard_map/ppermute | solution.py:25
  62.7 10.4 %collective-permute-start.4 = (bf16[8,768]{1,0:T(8,128)(2,1)S(1)}, bf16[8,768]{1,0:T(8,128)(2,1)S(1)}, u32[]{:S(2)}, u32[]{:S(2)}) collective-permute-start(bf16[8,768]{1,0:T(8,128)(2,1)S(1)} %broadcast_select_fusion.9), channel_id=1, source_target_pairs={{0,128},{8,136},{16,144},{24,152},{32,160},{40,168},{48,176},{56,1... | collective-permute-start | bytes 36872 | tf_op jit(solution)/shard_map/ppermute | solution.py:25
  65.1 31.8 %copy-start.17 = (bf16[8,768]{1,0:T(8,128)(2,1)}, bf16[8,768]{1,0:T(8,128)(2,1)S(1)}, u32[]{:S(2)}) copy-start(bf16[8,768]{1,0:T(8,128)(2,1)S(1)} %broadcast_select_fusion.4) | copy-start | bytes 36868
  65.2 14.0 %collective-permute-start.10 = (bf16[8,768]{1,0:T(8,128)(2,1)S(1)}, bf16[8,768]{1,0:T(8,128)(2,1)S(1)}, u32[]{:S(2)}, u32[]{:S(2)}) collective-permute-start(bf16[8,768]{1,0:T(8,128)(2,1)S(1)} %broadcast_select_fusion.4), channel_id=1, source_target_pairs={{0,256},{8,264},{16,272},{24,280},{32,288},{40,296},{48,304},{56,3... | collective-permute-start | bytes 36872 | tf_op jit(solution)/shard_map/ppermute | solution.py:25
  73.1 13.2 %collective-permute-start.5 = (bf16[8,768]{1,0:T(8,128)(2,1)S(1)}, bf16[8,768]{1,0:T(8,128)(2,1)S(1)}, u32[]{:S(2)}, u32[]{:S(2)}) collective-permute-start(bf16[8,768]{1,0:T(8,128)(2,1)S(1)} %broadcast_select_fusion.10), channel_id=1, source_target_pairs={{0,256},{8,264},{16,272},{24,280},{32,288},{40,296},{48,304},{56,3... | collective-permute-start | bytes 36872 | tf_op jit(solution)/shard_map/ppermute | solution.py:25
  87.3 19.1 %all-to-all-start.1 = ((bf16[8,8,512]{2,1,0:T(8,128)(2,1)}), bf16[8,8,512]{2,1,0:T(8,128)(2,1)S(1)}, u32[]{:S(2)}, u32[]{:S(2)}) async-start(bf16[8,8,512]{2,1,0:T(8,128)(2,1)} %broadcast_in_dim.16), calls=%async_computation.1 | async-start | bytes 131072 | tf_op jit(solution)/shard_map/all_to_all | solution.py:17
  107.0 13.7 %all-to-all-start.2 = ((bf16[8,8,512]{2,1,0:T(8,128)(2,1)}), bf16[8,8,512]{2,1,0:T(8,128)(2,1)}, u32[]{:S(2)}, u32[]{:S(2)}) async-start(bf16[8,8,512]{2,1,0:T(8,128)(2,1)} %broadcast_in_dim.17), calls=%async_computation.2 | async-start | bytes 131072 | tf_op jit(solution)/shard_map/all_to_all | solution.py:17
  129.7 14.7 %all-to-all-start.5 = ((bf16[8,8,512]{2,1,0:T(8,128)(2,1)}), bf16[8,8,512]{2,1,0:T(8,128)(2,1)S(1)}, u32[]{:S(2)}, u32[]{:S(2)}) async-start(bf16[8,8,512]{2,1,0:T(8,128)(2,1)} %fusion.5), calls=%async_computation.5 | async-start | bytes 131072 | tf_op jit(solution)/shard_map/all_to_all | solution.py:35
  144.4 13.7 %all-to-all-start.3 = ((bf16[8,8,512]{2,1,0:T(8,128)(2,1)}), bf16[8,8,512]{2,1,0:T(8,128)(2,1)S(1)}, u32[]{:S(2)}, u32[]{:S(2)}) async-start(bf16[8,8,512]{2,1,0:T(8,128)(2,1)} %fusion.4), calls=%async_computation.3 | async-start | bytes 131072 | tf_op jit(solution)/shard_map/all_to_all | solution.py:35
  158.1 13.0 %all-to-all-start.4 = ((bf16[8,8,512]{2,1,0:T(8,128)(2,1)}), bf16[8,8,512]{2,1,0:T(8,128)(2,1)S(1)}, u32[]{:S(2)}, u32[]{:S(2)}) async-start(bf16[8,8,512]{2,1,0:T(8,128)(2,1)} %fusion.3), calls=%async_computation.4 | async-start | bytes 131072 | tf_op jit(solution)/shard_map/all_to_all | solution.py:35
  161.5 504.7 %all-reduce.3.cloned.1.call-start = ((), (), s32[]{:S(2)}) async-start(), calls=%async_computation.6 | async-start | bytes 5242880 | tf_op jit(solution)/shard_map/psum | solution.py:170
  (36 other events, 297.3 us)
Sparse Core Ops, SparseCore 0:
  177.8 488.2 all-reduce.2
where the time goes:
time: 683 us; the launch traced here: 680 us
  waiting for transfers between devices  530 us (78%)
  starting transfers between devices  80.5 us (12%)
  matrix products  28.7 us (4%)
  between operations  23.9 us (3%)
  local copies, waits for them, and re-layouts  8.73 us (1%)
  other arithmetic  8.11 us (1%)
    psum x1, waiting for transfers between devices, per_device(): lax.psum((total_first, total_second), ('dom', 'grp'))  487 us
    ppermute x11, starting transfers between devices, partner_2(): lax.ppermute(value, axis, [(i, i ^ 1 << distance) for i in range(lax.axis...  48 us
    all_to_all x3, waiting for transfers between devices, summed_on_arrival(): lax.all_to_all(in_blocks(value, dim, length), axis, 0, 0, tiled=True)  22.6 us
    all_to_all x3, starting transfers between devices, from_everyone(): return lax.all_to_all(copies, axis, split_axis=0, concat_axis=0, tiled=True)  20.2 us
  transfers between devices with their start and end apart: 18, of which 8 were waited for; matrix products, arithmetic and copies ran while one was open for 3% of the time, Pallas kernels for 0%

commit v1 on v0

v1 whole, which is shorter than its diff:
```python
import functools
import math

import jax
import jax.numpy as jnp
from jax import lax
from jax.experimental import pallas as pl
from jax.experimental.pallas import tpu as pltpu
from jax.sharding import PartitionSpec as P

MESH = pl.DeviceIdType.MESH
BF = jnp.bfloat16
F32 = jnp.float32
HOP = 3


def mm(a, b):
    return jnp.dot(a, b, preferred_element_type=F32)


def nt(a, b):
    return lax.dot_general(a, b, (((1,), (1,)), ((), ())), preferred_element_type=F32)


def tn(a, b):
    return lax.dot_general(a, b, (((0,), (0,)), ((), ())), preferred_element_type=F32)


def sigmoid(v):
    return 1.0 / (1.0 + jnp.exp(-v))


def softplus(v):
    return jnp.maximum(v, 0.0) + jnp.log1p(jnp.exp(-jnp.abs(v)))


def body(
    dims,
    feat,
    w1_hbm,
    w2_hbm,
    table_hbm,
    heads,
    rels,
    tails,
    negs,
    partner,
    loss_out,
    g1_out,
    g2_out,
    w1,
    w2,
    table,
    ids,
    buf_y,
    send_x,
    buf_x,
    buf_z,
    buf_o,
    rel_rows,
    query,
    enc,
    slope,
    grads,
    dpre,
    xt,
    ht,
    core_send,
    core_recv,
    total,
    send_1,
    recv_1,
    part_2,
    send_2,
    recv_2,
    send_z,
    recv_z,
    gathered,
    squares,
    load_sem,
    send_sem,
    sem_y,
    sem_x,
    sem_z,
    sem_o,
    sem_core,
    sem_1,
    sem_2,
    sem_rz,
    sem_b,
    sem_a,
    sem_g,
    sem_s,
):
    nzh, na, ng = dims
    nz = nzh * ng
    rem, div = lax.rem, lax.div
    dom = lax.axis_index("dom")
    g = lax.axis_index("grp")
    c = rem(dom, 2)
    y = rem(div(dom, 2), na)
    x = rem(div(dom, 2 * na), na)
    zh = div(dom, 2 * na * na)
    z = zh * ng + g
    bits = na.bit_length() - 1

    def dev(zh_, x_, y_, c_, g_):
        return (((zh_ * na + x_) * na + y_) * 2 + c_, g_)

    def xor(v, k):
        out = 0
        for b in range(bits):
            out = out + rem(div(v, 1 << b) + (k >> b & 1), 2) * (1 << b)
        return out

    def on_ring(step):
        to = rem(z + step + nz, nz)
        return dev(div(to, ng), x, y, c, rem(to, ng))

    other_core = dev(zh, x, y, 1 - c, g)
    pending = []
    counter = [0]

    def push(src, dst, sem, target, keep=True):
        copy = pltpu.make_async_remote_copy(
            src_ref=src,
            dst_ref=dst,
            send_sem=send_sem.at[counter[0]],
            recv_sem=sem,
            device_id=target,
            device_id_type=MESH,
        )
        counter[0] += 1
        copy.start()
        if keep:
            pending.append(copy)
        return copy

    def arrived(dst, sem):
        pltpu.make_async_remote_copy(
            src_ref=dst,
            dst_ref=dst,
            send_sem=send_sem.at[0],
            recv_sem=sem,
            device_id=other_core,
            device_id_type=MESH,
        ).wait_recv()

    barrier = pltpu.get_barrier_semaphore()
    peers = [
        dev(zh, x, xor(y, k >> 1), rem(c + (k & 1), 2), g) for k in range(1, 2 * na)
    ]
    peers += [dev(zh, xor(x, k), y, c, g) for k in range(1, na)]
    peers += [on_ring(k) for k in range(1, nz)]
    peers += [dev(zh, x, y, 1 - c, rem(g + k, ng)) for k in range(1, ng)]
    for peer in peers:
        pl.semaphore_signal(barrier, inc=1, device_id=peer, device_id_type=MESH)

    loads = [
        pltpu.make_async_copy(table_hbm, table, load_sem.at[0]),
        pltpu.make_async_copy(w1_hbm, w1, load_sem.at[1]),
        pltpu.make_async_copy(w2_hbm, w2, load_sem.at[2]),
    ]
    for load in loads:
        load.start()
    buf_y[0] = feat[...]
    buf_o[g] = feat[...]
    ids[0:2] = heads[...].astype(F32)
    ids[2:4] = rels[...].astype(F32)
    ids[4:6] = tails[...].astype(F32)
    ids[6:8] = jnp.zeros_like(ids[6:8])
    pl.semaphore_wait(barrier, len(peers))

    for k in range(1, 2 * na):
        push(feat, buf_y.at[k], sem_y.at[k], dev(zh, x, xor(y, k >> 1), rem(c + (k & 1), 2), g))
    for k in range(1, ng):
        push(feat, buf_o.at[g], sem_o.at[g], dev(zh, x, y, c, rem(g + k, ng)))

    columns = jnp.transpose(ids[...])
    loads[0].wait()
    nrel = table.shape[0]
    edges = heads.shape[1]
    for r in range(2):
        pick = lax.broadcasted_iota(jnp.int32, (edges, nrel), 1).astype(F32) == columns[:, 2 + r : 3 + r]
        rel_rows[r] = mm(pick.astype(BF), table[...]).astype(BF)

    masks = [partner[r, 0] for r in range(2)]
    for k in range(1, 2 * na):
        arrived(buf_y.at[k], sem_y.at[k])
    for r in range(2):
        send_x[r] = buf_y[masks[r] % (2 * na)]
    for k in range(1, na):
        push(send_x, buf_x.at[k], sem_x.at[k], dev(zh, xor(x, k), y, c, g))
    buf_x[0] = send_x[...]
    for k in range(1, na):
        arrived(buf_x.at[k], sem_x.at[k])
    for r in range(2):
        buf_z[z, r] = buf_x[(masks[r] // (2 * na)) % na, r]

    reach = {1: nz // 2, -1: nz - 1 - nz // 2}
    seen = set()
    level = 0
    while HOP * level < reach[1]:
        for way in (1, -1):
            base = HOP * level
            if base >= reach[way]:
                continue
            source = rem(z - way * base + nz, nz)
            if level:
                arrived(buf_z.at[source], sem_z.at[source])
                seen.add(-way * base)
            for step in range(1, HOP + 1):
                if base + step <= reach[way]:
                    push(buf_z.at[source], buf_z.at[source], sem_z.at[source], on_ring(way * step))
        if level == 0:
            loads[1].wait()
            loads[2].wait()
            for k in range(1, ng):
                src = rem(g + k, ng)
                arrived(buf_o.at[src], sem_o.at[src])
            rows = 8 * ng
            half = w2.shape[1] // 2
            lane = lax.broadcasted_iota(jnp.int32, (edges, rows), 1).astype(F32)

            def encode(x_rows, first, count, at):
                pre = mm(x_rows, w1[...])
                s = sigmoid(pre)
                hidden = (pre * s).astype(BF)
                enc[first : first + count] = mm(hidden, w2[...]).astype(BF)
                slope[first : first + count] = s * (1.0 + pre * (1.0 - s))
                xt[:, at : at + count] = jnp.transpose(x_rows)
                ht[:, at : at + count] = jnp.transpose(hidden)

            own_x = buf_o[...].astype(F32).reshape(rows, feat.shape[1]).astype(BF)
            encode(own_x, 2 * rows, rows, 2 * rows)
            picks = []
            for r in range(2):
                head_pick = (lane == columns[:, r : r + 1]).astype(BF)
                picks.append(head_pick)
                head = mm(head_pick, enc[2 * rows : 3 * rows])
                rel = rel_rows[r].astype(F32)
                h_re, h_im = head[:, :half], head[:, half:]
                r_re, r_im = rel[:, :half], rel[:, half:]
                query[r, :, :half] = (h_re * r_re - h_im * r_im).astype(BF)
                query[r, :, half:] = (h_re * r_im + h_im * r_re).astype(BF)
            counts = []
            nneg = negs.shape[1]
            for r in range(2):
                hit = lax.broadcasted_iota(jnp.int32, (rows, nneg), 0) == negs[r : r + 1, :]
                counts.append(nt(jnp.ones((8, nneg), BF), hit.astype(F32).astype(BF))[0:1])
        level += 1
    for way in (1, -1):
        for dist in range(1, reach[way] + 1):
            if -way * dist not in seen:
                source = rem(z - way * dist + nz, nz)
                arrived(buf_z.at[source], sem_z.at[source])

    far = []
    for r in range(2):
        half_of = rem(zh + (masks[r] // (2 * na * na)) % 2, 2)
        rows_r = buf_z[pl.ds(half_of * ng, ng), r]
        far.append(rows_r.astype(F32).reshape(rows, feat.shape[1]))
    encode(jnp.concatenate(far, axis=0).astype(BF), 0, 2 * rows, 0)

    own = None
    losses = []
    for r in range(2):
        other = enc[r * rows : (r + 1) * rows]
        q = query[r]
        score = nt(q, other)
        tail_pick = jnp.where(lane == columns[:, 4 + r : 5 + r], 1.0, 0.0)
        positive = jnp.sum(score * tail_pick, axis=1, keepdims=True)
        losses.append(
            softplus(-positive) + jnp.sum(softplus(score) * counts[r], axis=1, keepdims=True) / nneg
        )
        weight_neg = (sigmoid(score) / nneg).astype(BF).astype(F32)
        weight_pos = -sigmoid(-positive)
        weight = (weight_neg * counts[r] + tail_pick * weight_pos).astype(BF)
        d_query = mm(weight, other)
        grads[r * rows : (r + 1) * rows] = tn(weight, q).astype(BF)
        rel = rel_rows[r].astype(F32)
        q_re, q_im = d_query[:, :half], d_query[:, half:]
        r_re, r_im = rel[:, :half], rel[:, half:]
        d_head = jnp.concatenate([q_re * r_re + q_im * r_im, q_im * r_re - q_re * r_im], axis=1)
        term = tn(picks[r], d_head.astype(BF))
        own = term if own is None else own + term
    grads[2 * rows : 3 * rows] = own.astype(BF)
    wide = lax.broadcasted_iota(jnp.int32, (edges, 128), 1)
    both = jnp.where(wide == 0, losses[0], jnp.where(wide == 1, losses[1], 0.0))
    loss_out[...] = jnp.transpose(both)[0:2]

    dpre[...] = (nt(grads[...], w2[...]) * slope[...]).astype(BF)
    rows_1, rows_2 = g1_out.shape[0], g2_out.shape[0]
    part_1, part_w2 = rows_1 // na, rows_2 // na
    block = part_1 + part_w2
    width = w2.shape[1] // na
    halves = ng // 2

    def slice_of(which, put):
        first_1 = pl.multiple_of(which * rows_1, rows_1)
        first_2 = pl.multiple_of(which * rows_2, rows_2)
        t1 = mm(xt[pl.ds(first_1, rows_1), 0 : 3 * rows], dpre[...])
        t2 = mm(ht[pl.ds(first_2, rows_2), 0 : 3 * rows], grads[...])
        for i in range(na):
            put(i, t2[i * part_w2 : (i + 1) * part_w2], t1[i * part_1 : (i + 1) * part_1])

    for gh in range(halves):

        def put_send(i, low, high, gh=gh):
            core_send[gh, i, 0:part_w2] = low.astype(BF)
            core_send[gh, i, part_w2:block] = high.astype(BF)

        slice_of(2 * gh + 1 - c, put_send)
        push(core_send.at[gh], core_recv.at[gh], sem_core.at[gh], other_core)
    for gh in range(halves):

        def put_own(i, low, high, gh=gh):
            total[gh, i, 0:part_w2] = low
            total[gh, i, part_w2:block] = high

        slice_of(2 * gh + c, put_own)

    a = c * x + (1 - c) * y
    b = c * y + (1 - c) * x

    def along_a(k):
        return dev(zh, c * k + (1 - c) * x, c * y + (1 - c) * k, c, g)

    def along_b(k):
        return dev(zh, c * x + (1 - c) * k, c * k + (1 - c) * y, c, g)

    for gh in range(halves):
        arrived(core_recv.at[gh], sem_core.at[gh])
        total[gh] = total[gh] + core_recv[gh].astype(F32)
        send_1[gh] = total[gh].astype(BF)
        for j in range(1, na):
            k = rem(a + j, na)
            push(send_1.at[gh, k], recv_1.at[a, gh], sem_1.at[a, gh], along_a(k))
    for gh in range(halves):
        part = total[gh, a]
        for j in range(1, na):
            k = rem(a + j, na)
            arrived(recv_1.at[k, gh], sem_1.at[k, gh])
            part = part + recv_1[k, gh].astype(F32)
        for i in range(na):
            part_2[i, gh] = part[:, i * width : (i + 1) * width]
            send_2[i, gh] = part[:, i * width : (i + 1) * width].astype(BF)
    for j in range(1, na):
        k = rem(b + j, na)
        push(send_2.at[k], recv_2.at[b], sem_2.at[b], along_b(k))
    part = part_2[b]
    for j in range(1, na):
        k = rem(b + j, na)
        arrived(recv_2.at[k], sem_2.at[k])
        part = part + recv_2[k].astype(F32)
    send_z[...] = part.astype(BF)

    matched = rem(g + c, 2) == 0
    conditional = []
    for gh in range(halves):
        for zp in range(nzh):
            to = 2 * gh + c
            elsewhere = jnp.logical_or(rem(zh + zp, nzh) != zh, to != g)
            conditional.append((elsewhere, gh, zp, counter[0]))

            @pl.when(elsewhere)
            def _(gh=gh, zp=zp, to=to):
                push(
                    send_z.at[gh],
                    recv_z.at[z],
                    sem_rz.at[z],
                    dev(rem(zh + zp, nzh), x, y, c, to),
                    keep=False,
                )

    base_s = counter[0]

    @pl.when(matched)
    def _():
        recv_z[z] = send_z[div(g, 2)]
        for k in range(1, nz):
            source = rem(z + k, nz)
            arrived(recv_z.at[source], sem_rz.at[source])
        piece = jnp.zeros((block, width), F32)
        for k in range(nz):
            piece = piece + recv_z[k].astype(F32)
        gathered[a, b, 0:block] = piece
        gathered[a, b, block : block + 8] = jnp.full((8, width), jnp.sum(piece * piece), F32)
        mine = []
        for j in range(1, na):
            mine.append(
                push(
                    gathered.at[a, b],
                    gathered.at[a, b],
                    sem_b.at[b],
                    along_b(rem(b + j, na)),
                    keep=False,
                )
            )
        for j in range(1, na):
            k = rem(b + j, na)
            arrived(gathered.at[a, k], sem_b.at[k])
        for j in range(1, na):
            mine.append(
                push(
                    gathered.at[a],
                    gathered.at[a],
                    sem_a.at[a],
                    along_a(rem(a + j, na)),
                    keep=False,
                )
            )
        mine.append(push(gathered.at[a], gathered.at[a], sem_g.at[a], other_core, keep=False))
        for j in range(1, na):
            k = rem(a + j, na)
            arrived(gathered.at[k], sem_a.at[k])
            mine.append(push(gathered.at[k], gathered.at[k], sem_g.at[k], other_core, keep=False))
        ss = jnp.zeros((8, width), F32)
        for i in range(na):
            for k in range(na):
                ss = ss + gathered[i, k, block : block + 8]
        squares[g] = ss
        for k in range(1, ng):
            for cc in range(2):
                mine.append(
                    push(
                        squares.at[g],
                        squares.at[g],
                        sem_s.at[g],
                        dev(zh, x, y, cc, rem(g + k, ng)),
                        keep=False,
                    )
                )
        mine.append(push(squares.at[g], squares.at[g], sem_s.at[g], other_core, keep=False))
        for copy in mine:
            copy.wait_send()

    @pl.when(jnp.logical_not(matched))
    def _():
        arrived(squares.at[g], sem_s.at[g])
        for k in range(na):
            arrived(gathered.at[k], sem_g.at[k])

    for k in range(1, ng):
        source = rem(g + k, ng)
        arrived(squares.at[source], sem_s.at[source])
    ss = squares[0]
    for k in range(1, ng):
        ss = ss + squares[k]
    count = float(ng * block * na * na * width)
    factor = jnp.minimum(1.0, math.sqrt(count) / jnp.sqrt(ss + 1e-06))[0:1]
    for i in range(na):
        for k in range(na):
            g2_out[i * part_w2 : (i + 1) * part_w2, k * width : (k + 1) * width] = (
                gathered[i, k, 0:part_w2] * factor
            )
            g1_out[i * part_1 : (i + 1) * part_1, k * width : (k + 1) * width] = (
                gathered[i, k, part_w2:block] * factor
            )

    for copy in pending:
        copy.wait_send()
    for elsewhere, gh, zp, index in conditional:

        @pl.when(elsewhere)
        def _(gh=gh, zp=zp, index=index):
            pltpu.make_async_remote_copy(
                src_ref=send_z.at[gh],
                dst_ref=recv_z.at[z],
                send_sem=send_sem.at[index],
                recv_sem=sem_rz.at[z],
                device_id=dev(rem(zh + zp, nzh), x, y, c, 2 * gh + c),
                device_id_type=MESH,
            ).wait_send()


def per_device(dims, features, w_first, w_second, table, heads, relations, tails, negatives, partner):
    nzh, na, ng = dims
    nz = nzh * ng
    own, d_in = features.shape
    d_hid, d_enc = w_second.shape
    edges = heads.shape[1]
    rows = own * ng
    rows_1, rows_2 = d_in // ng, d_hid // ng
    block, width, halves = (rows_1 + rows_2) // na, d_enc // na, ng // 2
    lanes = max(256, 3 * rows)
    vmem = pl.BlockSpec(memory_space=pltpu.VMEM)
    anyspace = pl.BlockSpec(memory_space=pl.ANY)
    smem = pl.BlockSpec(memory_space=pltpu.SMEM)
    V, S = pltpu.VMEM, pltpu.SemaphoreType.DMA
    return pl.pallas_call(
        functools.partial(body, dims),
        out_shape=(
            jax.ShapeDtypeStruct(heads.shape, F32),
            jax.ShapeDtypeStruct((rows_1, d_hid), F32),
            jax.ShapeDtypeStruct((rows_2, d_enc), F32),
        ),
        in_specs=[vmem, anyspace, anyspace, anyspace, vmem, vmem, vmem, vmem, smem],
        out_specs=(vmem, vmem, vmem),
        scratch_shapes=[
            V(w_first.shape, BF),
            V(w_second.shape, BF),
            V(table.shape, BF),
            V((8, edges), F32),
            V((2 * na, own, d_in), BF),
            V((2, own, d_in), BF),
            V((na, 2, own, d_in), BF),
            V((nz, 2, own, d_in), BF),
            V((ng, own, d_in), BF),
            V((2, edges, d_enc), BF),
            V((2, edges, d_enc), BF),
            V((3 * rows, d_enc), BF),
            V((3 * rows, d_hid), F32),
            V((3 * rows, d_enc), BF),
            V((3 * rows, d_hid), BF),
            V((d_in, lanes), BF),
            V((d_hid, lanes), BF),
            V((halves, na, block, d_enc), BF),
            V((halves, na, block, d_enc), BF),
            V((halves, na, block, d_enc), F32),
            V((halves, na, block, d_enc), BF),
            V((na, halves, block, d_enc), BF),
            V((na, halves, block, width), F32),
            V((na, halves, block, width), BF),
            V((na, halves, block, width), BF),
            V((halves, block, width), BF),
            V((nz, block, width), BF),
            V((na, na, block + 8, width), F32),
            V((ng, 8, width), F32),
            S((3,)),
            S((128,)),
            S((2 * na,)),
            S((na,)),
            S((nz,)),
            S((ng,)),
            S((halves,)),
            S((na, halves)),
            S((na,)),
            S((nz,)),
            S((na,)),
            S((na,)),
            S((na,)),
            S((ng,)),
        ],
        compiler_params=pltpu.CompilerParams(
            collective_id=0, has_side_effects=True, vmem_limit_bytes=56 * 1024 * 1024
        ),
        name="step",
    )(features, w_first, w_second, table, heads, relations, tails, negatives, partner)


def solution(mesh):
    ng = mesh.shape["grp"]
    na = math.isqrt(mesh.shape["dom"] // 4)
    return jax.shard_map(
        functools.partial(per_device, (2, na, ng)),
        mesh=mesh,
        in_specs=(
            P(("dom", "grp"), None),
            P(),
            P(),
            P(),
            P(None, ("dom", "grp")),
            P(None, ("dom", "grp")),
            P(None, ("dom", "grp")),
            P(),
            P(),
        ),
        out_specs=(P(None, ("dom", "grp")), P("grp", None), P("grp", None)),
        check_vma=False,
    )
```

time: 683 us -> 86.7 us (0.13)
  waiting for transfers between devices: 530 us -> 0 us
  Pallas kernels: 0 us -> 81.4 us
  starting transfers between devices: 80.5 us -> 0 us
  matrix products: 28.7 us -> 0 us
  between operations: 23.9 us -> 0.64 us
  other arithmetic: 8.11 us -> 0 us
    psum x1 -> x0, waiting for transfers between devices: 487 us -> none  [per_device(): lax.psum((total_first, total_second), ('dom', 'grp'))]
    pallas_call x0 -> x1, Pallas kernels: none -> 81.4 us  [per_device(): pl.pallas_call(functools.partial(body, dims), out_shape=(jax.ShapeDtypeSt...]
    ppermute x11 -> x0, starting transfers between devices: 48 us -> none  [partner_2(): lax.ppermute(value, axis, [(i, i ^ 1 << distance) for i in range(lax.axis...]
    all_to_all x6 -> x0, waiting for transfers between devices: 35.4 us -> none  [the longest x3 22.6 us: summed_on_arrival(): lax.all_to_all(in_blocks(value, dim, length), axis, 0, 0, tiled=True)]
    all_to_all x6 -> x0, starting transfers between devices: 32.5 us -> none  [the longest x3 20.2 us: from_everyone(): return lax.all_to_all(copies, axis, split_axis=0, concat_axis=0, tiled=True)]
    dot_general x30 -> x0, matrix products: 28.7 us -> none  [the longest x6 7.6 us: add_into_rows(): lax.dot_general(selector.astype(jnp.float32), values, (((0,), (0,)), ((),...]
    ppermute x11 -> x0, waiting for transfers between devices: 7.47 us -> none  [partner_2(): lax.ppermute(value, axis, [(i, i ^ 1 << distance) for i in range(lax.axis...]
  transfers between devices with their start and end apart: 18 -> 0, of which waited for: 8 -> 0; matrix products, arithmetic and copies ran while one was open for 3% -> 0% of each run, Pallas kernels for 0% -> 0%
where the time goes in v1:
time: 86.7 us; the launch traced here: 86.5 us
  Pallas kernels  81.4 us (94%)
  local copies, waits for them, and re-layouts  4.42 us (5%)
    pallas_call x1, Pallas kernels, per_device(): pl.pallas_call(functools.partial(body, dims), out_shape=(jax.ShapeDtypeSt...  81.4 us
    unnamed x3, local copies, waits for them, and re-layouts  4.42 us

profile of v1, /device:TPU:1, one launch (start us, length us, event | category | flops | bytes accessed | tf_op | source)
XLA Modules:
  0.0 86.5 jit_solution(17055514963227159593)
XLA Ops:
  0.6 81.4 %step.1 = (f32[2,128]{1,0:T(2,128)}, f32[96,512]{1,0:T(8,128)}, f32[64,512]{1,0:T(8,128)}) custom-call(bf16[8,768]{1,0:T(8,128)(2,1)} %feat.1, bf16[768,512]{1,0:T(8,128)(2,1)} %w1_hbm.1, bf16[512,512]{1,0:T(8,128)(2,1)} %w2_hbm.1, bf16[1387,512]{1,0:T(8,128)(2,1)} %table_hbm.1, s32[2,128]{1,0:T(2,128)} %heads.1, s32[2,128]{1,0:T(2,128)} %rels.1, ...), custom_call_target="tpu_custom_call" | custom-call | tf_op jit(solution)/shard_map/step/pallas_call | solution.py:491
  82.1 1.2 %copy.15 = f32[2,128]{1,0:T(2,128)} copy(f32[2,128]{1,0:T(2,128)} %get-tuple-element.6) | data formatting | bytes 2048
  83.3 1.6 %copy.16 = f32[96,512]{1,0:T(8,128)} copy(f32[96,512]{1,0:T(8,128)} %get-tuple-element.7) | data formatting | bytes 393216
  84.9 1.6 %copy.17 = f32[64,512]{1,0:T(8,128)} copy(f32[64,512]{1,0:T(8,128)} %get-tuple-element.8) | data formatting | bytes 262144

commit v2 on v1

--- a/solution.py
+++ b/solution.py
@@ -36,21 +36,27 @@
 
 def body(
     dims,
-    feat,
+    feat_hbm,
     w1_hbm,
     w2_hbm,
     table_hbm,
+    heads_hbm,
+    rels_hbm,
+    tails_hbm,
+    negs_hbm,
+    partner_hbm,
+    loss_out,
+    gathered,
+    norm_out,
+    feat,
+    w1,
+    w2,
+    table,
     heads,
     rels,
     tails,
     negs,
     partner,
-    loss_out,
-    g1_out,
-    g2_out,
-    w1,
-    w2,
-    table,
     ids,
     buf_y,
     send_x,
@@ -75,7 +81,7 @@
     recv_2,
     send_z,
     recv_z,
-    gathered,
+    parts_sq,
     squares,
     load_sem,
     send_sem,
@@ -87,9 +93,9 @@
     sem_1,
     sem_2,
     sem_rz,
-    sem_b,
-    sem_a,
-    sem_g,
+    sem_q,
+    sem_p,
+    sem_c,
     sem_s,
 ):
     nzh, na, ng = dims
@@ -146,38 +152,69 @@
             device_id_type=MESH,
         ).wait_recv()
 
+    def ring(buf, sem):
+        reach = {1: nz // 2, -1: nz - 1 - nz // 2}
+        seen = set()
+        for base in range(0, reach[1], HOP):
+            for way in (1, -1):
+                if base >= reach[way]:
+                    continue
+                source = rem(z - way * base + nz, nz)
+                if base:
+                    arrived(buf.at[source], sem.at[source])
+                    seen.add(-way * base)
+                for step in range(min(HOP, reach[way] - base), 0, -1):
+                    push(buf.at[source], buf.at[source], sem.at[source], on_ring(way * step))
+            yield
+        for way in (1, -1):
+            for dist in range(1, reach[way] + 1):
+                if -way * dist not in seen:
+                    source = rem(z - way * dist + nz, nz)
+                    arrived(buf.at[source], sem.at[source])
+
     barrier = pltpu.get_barrier_semaphore()
     peers = [
         dev(zh, x, xor(y, k >> 1), rem(c + (k & 1), 2), g) for k in range(1, 2 * na)
     ]
     peers += [dev(zh, xor(x, k), y, c, g) for k in range(1, na)]
-    peers += [on_ring(k) for k in range(1, nz)]
-    peers += [dev(zh, x, y, 1 - c, rem(g + k, ng)) for k in range(1, ng)]
+    near = min(HOP, nz // 2)
+    peers += [on_ring(k) for k in range(1, nz) if min(k, nz - k) <= near]
     for peer in peers:
         pl.semaphore_signal(barrier, inc=1, device_id=peer, device_id_type=MESH)
 
-    loads = [
-        pltpu.make_async_copy(table_hbm, table, load_sem.at[0]),
-        pltpu.make_async_copy(w1_hbm, w1, load_sem.at[1]),
-        pltpu.make_async_copy(w2_hbm, w2, load_sem.at[2]),
-    ]
-    for load in loads:
-        load.start()
-    buf_y[0] = feat[...]
-    buf_o[g] = feat[...]
+    pairs = (
+        (feat_hbm, feat),
+        (feat_hbm, buf_y.at[0]),
+        (feat_hbm, buf_o.at[z]),
+        (partner_hbm, partner),
+        (heads_hbm, heads),
+        (rels_hbm, rels),
+        (tails_hbm, tails),
+        (negs_hbm, negs),
+        (table_hbm, table),
+        (w1_hbm, w1),
+        (w2_hbm, w2),
+    )
+    loads = []
+    for i, (src, dst) in enumerate(pairs):
+        loads.append(pltpu.make_async_copy(src, dst, load_sem.at[i]))
+        loads[-1].start()
+    for load in loads[0:3]:
+        load.wait()
+    pl.semaphore_wait(barrier, len(peers))
+
+    for k in range(1, 2 * na):
+        push(feat, buf_y.at[k], sem_y.at[k], dev(zh, x, xor(y, k >> 1), rem(c + (k & 1), 2), g))
+    own_ring = ring(buf_o, sem_o)
+    next(own_ring)
+
+    for load in loads[3:9]:
+        load.wait()
     ids[0:2] = heads[...].astype(F32)
     ids[2:4] = rels[...].astype(F32)
     ids[4:6] = tails[...].astype(F32)
     ids[6:8] = jnp.zeros_like(ids[6:8])
-    pl.semaphore_wait(barrier, len(peers))
-
-    for k in range(1, 2 * na):
-        push(feat, buf_y.at[k], sem_y.at[k], dev(zh, x, xor(y, k >> 1), rem(c + (k & 1), 2), g))
-    for k in range(1, ng):
-        push(feat, buf_o.at[g], sem_o.at[g], dev(zh, x, y, c, rem(g + k, ng)))
-
     columns = jnp.transpose(ids[...])
-    loads[0].wait()
     nrel = table.shape[0]
     edges = heads.shape[1]
     for r in range(2):
@@ -191,69 +228,52 @@
         send_x[r] = buf_y[masks[r] % (2 * na)]
     for k in range(1, na):
         push(send_x, buf_x.at[k], sem_x.at[k], dev(zh, xor(x, k), y, c, g))
+    next(own_ring, None)
     buf_x[0] = send_x[...]
     for k in range(1, na):
         arrived(buf_x.at[k], sem_x.at[k])
     for r in range(2):
         buf_z[z, r] = buf_x[(masks[r] // (2 * na)) % na, r]
 
-    reach = {1: nz // 2, -1: nz - 1 - nz // 2}
-    seen = set()
-    level = 0
-    while HOP * level < reach[1]:
-        for way in (1, -1):
-            base = HOP * level
-            if base >= reach[way]:
-                continue
-            source = rem(z - way * base + nz, nz)
-            if level:
-                arrived(buf_z.at[source], sem_z.at[source])
-                seen.add(-way * base)
-            for step in range(1, HOP + 1):
-                if base + step <= reach[way]:
-                    push(buf_z.at[source], buf_z.at[source], sem_z.at[source], on_ring(way * step))
-        if level == 0:
-            loads[1].wait()
-            loads[2].wait()
-            for k in range(1, ng):
-                src = rem(g + k, ng)
-                arrived(buf_o.at[src], sem_o.at[src])
-            rows = 8 * ng
-            half = w2.shape[1] // 2
-            lane = lax.broadcasted_iota(jnp.int32, (edges, rows), 1).astype(F32)
-
-            def encode(x_rows, first, count, at):
-                pre = mm(x_rows, w1[...])
-                s = sigmoid(pre)
-                hidden = (pre * s).astype(BF)
-                enc[first : first + count] = mm(hidden, w2[...]).astype(BF)
-                slope[first : first + count] = s * (1.0 + pre * (1.0 - s))
-                xt[:, at : at + count] = jnp.transpose(x_rows)
-                ht[:, at : at + count] = jnp.transpose(hidden)
-
-            own_x = buf_o[...].astype(F32).reshape(rows, feat.shape[1]).astype(BF)
-            encode(own_x, 2 * rows, rows, 2 * rows)
-            picks = []
-            for r in range(2):
-                head_pick = (lane == columns[:, r : r + 1]).astype(BF)
-                picks.append(head_pick)
-                head = mm(head_pick, enc[2 * rows : 3 * rows])
-                rel = rel_rows[r].astype(F32)
-                h_re, h_im = head[:, :half], head[:, half:]
-                r_re, r_im = rel[:, :half], rel[:, half:]
-                query[r, :, :half] = (h_re * r_re - h_im * r_im).astype(BF)
-                query[r, :, half:] = (h_re * r_im + h_im * r_re).astype(BF)
-            counts = []
-            nneg = negs.shape[1]
-            for r in range(2):
-                hit = lax.broadcasted_iota(jnp.int32, (rows, nneg), 0) == negs[r : r + 1, :]
-                counts.append(nt(jnp.ones((8, nneg), BF), hit.astype(F32).astype(BF))[0:1])
-        level += 1
-    for way in (1, -1):
-        for dist in range(1, reach[way] + 1):
-            if -way * dist not in seen:
-                source = rem(z - way * dist + nz, nz)
-                arrived(buf_z.at[source], sem_z.at[source])
+    far_ring = ring(buf_z, sem_z)
+    next(far_ring)
+    for _ in own_ring:
+        pass
+
+    for load in loads[9:]:
+        load.wait()
+    rows = 8 * ng
+    half = w2.shape[1] // 2
+    lane = lax.broadcasted_iota(jnp.int32, (edges, rows), 1).astype(F32)
+
+    def encode(x_rows, first, count, at):
+        pre = mm(x_rows, w1[...])
+        s = sigmoid(pre)
+        hidden = (pre * s).astype(BF)
+        enc[first : first + count] = mm(hidden, w2[...]).astype(BF)
+        slope[first : first + count] = s * (1.0 + pre * (1.0 - s))
+        xt[:, at : at + count] = jnp.transpose(x_rows)
+        ht[:, at : at + count] = jnp.transpose(hidden)
+
+    own_x = buf_o[pl.ds(zh * ng, ng)].astype(F32).reshape(rows, feat.shape[1]).astype(BF)
+    encode(own_x, 2 * rows, rows, 2 * rows)
+    picks = []
+    for r in range(2):
+        head_pick = (lane == columns[:, r : r + 1]).astype(BF)
+        picks.append(head_pick)
+        head = mm(head_pick, enc[2 * rows : 3 * rows])
+        rel = rel_rows[r].astype(F32)
+        h_re, h_im = head[:, :half], head[:, half:]
+        r_re, r_im = rel[:, :half], rel[:, half:]
+        query[r, :, :half] = (h_re * r_re - h_im * r_im).astype(BF)
+        query[r, :, half:] = (h_re * r_im + h_im * r_re).astype(BF)
+    counts = []
+    nneg = negs.shape[1]
+    for r in range(2):
+        hit = lax.broadcasted_iota(jnp.int32, (rows, nneg), 0) == negs[r : r + 1, :]
+        counts.append(nt(jnp.ones((8, nneg), BF), hit.astype(F32).astype(BF))[0:1])
+    for _ in far_ring:
+        pass
 
     far = []
     for r in range(2):
@@ -290,7 +310,7 @@
     loss_out[...] = jnp.transpose(both)[0:2]
 
     dpre[...] = (nt(grads[...], w2[...]) * slope[...]).astype(BF)
-    rows_1, rows_2 = g1_out.shape[0], g2_out.shape[0]
+    rows_1, rows_2 = w1.shape[0] // ng, w2.shape[0] // ng
     part_1, part_w2 = rows_1 // na, rows_2 // na
     block = part_1 + part_w2
     width = w2.shape[1] // na
@@ -325,6 +345,10 @@
 
     def along_a(k):
         return dev(zh, c * k + (1 - c) * x, c * y + (1 - c) * k, c, g)
+
+    def in_plane(k):
+        ka, kb = div(k, na), rem(k, na)
+        return dev(zh, c * ka + (1 - c) * kb, c * kb + (1 - c) * ka, c, g)
 
     def along_b(k):
         return dev(zh, c * x + (1 - c) * k, c * k + (1 - c) * y, c, g)
@@ -373,8 +397,6 @@
                     keep=False,
                 )
 
-    base_s = counter[0]
-
     @pl.when(matched)
     def _():
         recv_z[z] = send_z[div(g, 2)]
@@ -384,43 +406,30 @@
         piece = jnp.zeros((block, width), F32)
         for k in range(nz):
             piece = piece + recv_z[k].astype(F32)
-        gathered[a, b, 0:block] = piece
-        gathered[a, b, block : block + 8] = jnp.full((8, width), jnp.sum(piece * piece), F32)
+        slot = a * na + b
+        places = na * na
+        parts_sq[slot] = jnp.full((1, width), jnp.sum(piece * piece), F32)
         mine = []
-        for j in range(1, na):
+        for t in range(1, places):
+            to = rem(slot + t, places)
             mine.append(
-                push(
-                    gathered.at[a, b],
-                    gathered.at[a, b],
-                    sem_b.at[b],
-                    along_b(rem(b + j, na)),
-                    keep=False,
-                )
+                push(parts_sq.at[slot], parts_sq.at[slot], sem_q.at[slot], in_plane(to), keep=False)
             )
-        for j in range(1, na):
-            k = rem(b + j, na)
-            arrived(gathered.at[a, k], sem_b.at[k])
-        for j in range(1, na):
+        gathered[slot] = piece
+        for t in range(1, places):
+            to = rem(slot + t, places)
             mine.append(
-                push(
-                    gathered.at[a],
-                    gathered.at[a],
-                    sem_a.at[a],
-                    along_a(rem(a + j, na)),
-                    keep=False,
-                )
+                push(gathered.at[slot], gathered.at[slot], sem_p.at[slot], in_plane(to), keep=False)
             )
-        mine.append(push(gathered.at[a], gathered.at[a], sem_g.at[a], other_core, keep=False))
-        for j in range(1, na):
-            k = rem(a + j, na)
-            arrived(gathered.at[k], sem_a.at[k])
-            mine.append(push(gathered.at[k], gathered.at[k], sem_g.at[k], other_core, keep=False))
-        ss = jnp.zeros((8, width), F32)
-        for i in range(na):
-            for k in range(na):
-                ss = ss + gathered[i, k, block : block + 8]
+        mine.append(push(gathered.at[slot], gathered.at[slot], sem_c.at[slot], other_core, keep=False))
+        for t in range(1, places):
+            source = rem(slot + t, places)
+            arrived(parts_sq.at[source], sem_q.at[source])
+        ss = parts_sq[0]
+        for i in range(1, places):
+            ss = ss + parts_sq[i]
         squares[g] = ss
-        for k in range(1, ng):
+        for k in range(ng - 1, 0, -1):
             for cc in range(2):
                 mine.append(
                     push(
@@ -432,14 +441,20 @@
                     )
                 )
         mine.append(push(squares.at[g], squares.at[g], sem_s.at[g], other_core, keep=False))
+        for t in range(places - 1, 0, -1):
+            source = rem(slot + t, places)
+            arrived(gathered.at[source], sem_p.at[source])
+            mine.append(
+                push(gathered.at[source], gathered.at[source], sem_c.at[source], other_core, keep=False)
+            )
         for copy in mine:
             copy.wait_send()
 
     @pl.when(jnp.logical_not(matched))
     def _():
         arrived(squares.at[g], sem_s.at[g])
-        for k in range(na):
-            arrived(gathered.at[k], sem_g.at[k])
+        for k in range(na * na):
+            arrived(gathered.at[k], sem_c.at[k])
 
     for k in range(1, ng):
         source = rem(g + k, ng)
@@ -447,16 +462,7 @@
     ss = squares[0]
     for k in range(1, ng):
         ss = ss + squares[k]
-    count = float(ng * block * na * na * width)
-    factor = jnp.minimum(1.0, math.sqrt(count) / jnp.sqrt(ss + 1e-06))[0:1]
-    for i in range(na):
-        for k in range(na):
-            g2_out[i * part_w2 : (i + 1) * part_w2, k * width : (k + 1) * width] = (
-                gathered[i, k, 0:part_w2] * factor
-            )
-            g1_out[i * part_1 : (i + 1) * part_1, k * width : (k + 1) * width] = (
-                gathered[i, k, part_w2:block] * factor
-            )
+    norm_out[...] = ss
 
     for copy in pending:
         copy.wait_send()
@@ -472,6 +478,19 @@
                 device_id=dev(rem(zh + zp, nzh), x, y, c, 2 * gh + c),
                 device_id_type=MESH,
             ).wait_send()
+
+
+def finish(na, count, loss_in, pieces, squares, loss_out, g1_out, g2_out):
+    low = g2_out.shape[0] // na
+    high = g1_out.shape[0] // na
+    width = pieces.shape[2]
+    factor = jnp.minimum(1.0, math.sqrt(count) / jnp.sqrt(squares[...] + 1e-06))
+    loss_out[...] = loss_in[...]
+    for i in range(na):
+        for k in range(na):
+            column = slice(k * width, (k + 1) * width)
+            g2_out[i * low : (i + 1) * low, column] = pieces[i * na + k, 0:low] * factor
+            g1_out[i * high : (i + 1) * high, column] = pieces[i * na + k, low:] * factor
 
 
 def per_device(dims, features, w_first, w_second, table, heads, relations, tails, negatives, partner):
@@ -485,28 +504,33 @@
     block, width, halves = (rows_1 + rows_2) // na, d_enc // na, ng // 2
     lanes = max(256, 3 * rows)
     vmem = pl.BlockSpec(memory_space=pltpu.VMEM)
-    anyspace = pl.BlockSpec(memory_space=pl.ANY)
-    smem = pl.BlockSpec(memory_space=pltpu.SMEM)
+    hbm = pl.BlockSpec(memory_space=pltpu.HBM)
     V, S = pltpu.VMEM, pltpu.SemaphoreType.DMA
-    return pl.pallas_call(
+    loss, pieces, squares = pl.pallas_call(
         functools.partial(body, dims),
         out_shape=(
             jax.ShapeDtypeStruct(heads.shape, F32),
-            jax.ShapeDtypeStruct((rows_1, d_hid), F32),
-            jax.ShapeDtypeStruct((rows_2, d_enc), F32),
+            jax.ShapeDtypeStruct((na * na, block, width), F32),
+            jax.ShapeDtypeStruct((1, width), F32),
         ),
-        in_specs=[vmem, anyspace, anyspace, anyspace, vmem, vmem, vmem, vmem, smem],
+        in_specs=[hbm] * 9,
         out_specs=(vmem, vmem, vmem),
         scratch_shapes=[
+            V(features.shape, BF),
             V(w_first.shape, BF),
             V(w_second.shape, BF),
             V(table.shape, BF),
+            V(heads.shape, jnp.int32),
+            V(relations.shape, jnp.int32),
+            V(tails.shape, jnp.int32),
+            V(negatives.shape, jnp.int32),
+            pltpu.SMEM(partner.shape, jnp.int32),
             V((8, edges), F32),
             V((2 * na, own, d_in), BF),
             V((2, own, d_in), BF),
             V((na, 2, own, d_in), BF),
             V((nz, 2, own, d_in), BF),
-            V((ng, own, d_in), BF),
+            V((nz, own, d_in), BF),
             V((2, edges, d_enc), BF),
             V((2, edges, d_enc), BF),
             V((3 * rows, d_enc), BF),
@@ -525,28 +549,39 @@
             V((na, halves, block, width), BF),
             V((halves, block, width), BF),
             V((nz, block, width), BF),
-            V((na, na, block + 8, width), F32),
-            V((ng, 8, width), F32),
-            S((3,)),
-            S((128,)),
+            V((na * na, 1, width), F32),
+            V((ng, 1, width), F32),
+            S((11,)),
+            S((160,)),
             S((2 * na,)),
             S((na,)),
             S((nz,)),
-            S((ng,)),
+            S((nz,)),
             S((halves,)),
             S((na, halves)),
             S((na,)),
             S((nz,)),
-            S((na,)),
-            S((na,)),
-            S((na,)),
+            S((na * na,)),
+            S((na * na,)),
+            S((na * na,)),
             S((ng,)),
         ],
         compiler_params=pltpu.CompilerParams(
-            collective_id=0, has_side_effects=True, vmem_limit_bytes=56 * 1024 * 1024
+            collective_id=0, has_side_effects=True, vmem_limit_bytes=24 * 1024 * 1024
         ),
         name="step",
     )(features, w_first, w_second, table, heads, relations, tails, negatives, partner)
+    return pl.pallas_call(
+        functools.partial(finish, na, float(w_first.size + w_second.size)),
+        out_shape=(
+            jax.ShapeDtypeStruct(heads.shape, F32),
+            jax.ShapeDtypeStruct((rows_1, d_hid), F32),
+            jax.ShapeDtypeStruct((rows_2, d_enc), F32),
+        ),
+        in_specs=[vmem] * 3,
+        out_specs=(vmem, vmem, vmem),
+        name="finish",
+    )(loss, pieces, squares)
 
 
 def solution(mesh):

time: 86.7 us -> 84.6 us (0.976)
  Pallas kernels: 81.4 us -> 74.1 us
  local copies, waits for them, and re-layouts: 4.42 us -> 9.47 us
    pallas_call x1, Pallas kernels: 81.4 us -> 72.4 us  [per_device(): pl.pallas_call(functools.partial(body, dims), out_shape=(jax.ShapeDtypeSt...]
    unnamed x3 -> x24, local copies, waits for them, and re-layouts: 4.42 us -> 9.47 us
    pallas_call x0 -> x1, Pallas kernels: none -> 1.72 us  [per_device(): pl.pallas_call(functools.partial(finish, na, float(w_first.size + w_secon...]
where the time goes in v2:
time: 84.6 us; the launch traced here: 84.2 us
  Pallas kernels  74.1 us (88%)
  local copies, waits for them, and re-layouts  9.47 us (11%)
    pallas_call x1, Pallas kernels, per_device(): pl.pallas_call(functools.partial(body, dims), out_shape=(jax.ShapeDtypeSt...  72.4 us
    unnamed x24, local copies, waits for them, and re-layouts  9.47 us
    pallas_call x1, Pallas kernels, per_device(): pl.pallas_call(functools.partial(finish, na, float(w_first.size + w_secon...  1.72 us

profile of v2, /device:TPU:1, one launch (start us, length us, event | category | flops | bytes accessed | tf_op | source)
XLA Modules:
  0.0 84.2 jit_solution(401271450512799160)
XLA Ops:
  0.6 0.0 copy-start
  0.6 1.3 %copy-done = bf16[1387,512]{1,0:T(8,128)(2,1)S(1)} copy-done((bf16[1387,512]{1,0:T(8,128)(2,1)S(1)}, bf16[1387,512]{1,0:T(8,128)(2,1)}, u32[]{:S(2)}) %copy-start) | copy-done | bytes 1420312
  2.0 0.0 copy-start.1
  2.0 1.1 %copy-done.1 = bf16[768,512]{1,0:T(8,128)(2,1)S(1)} copy-done((bf16[768,512]{1,0:T(8,128)(2,1)S(1)}, bf16[768,512]{1,0:T(8,128)(2,1)}, u32[]{:S(2)}) %copy-start.1) | copy-done | bytes 786456
  3.1 0.0 copy-start.2
  3.1 1.0 %copy-done.2 = bf16[512,512]{1,0:T(8,128)(2,1)S(1)} copy-done((bf16[512,512]{1,0:T(8,128)(2,1)S(1)}, bf16[512,512]{1,0:T(8,128)(2,1)}, u32[]{:S(2)}) %copy-start.2) | copy-done | bytes 524312
  4.2 0.0 copy-start.4
  4.2 0.7 copy-done.4
  4.9 0.0 copy-start.5
  4.9 0.7 copy-done.5
  5.6 0.0 copy-start.6
  5.6 0.7 copy-done.6
  6.2 0.0 copy-start.7
  6.2 0.7 copy-done.7
  6.9 0.0 copy-start.8
  6.9 0.7 copy-done.8
  7.6 0.0 copy-start.9
  7.6 0.7 copy-done.9
  8.3 72.4 %step.1 = (f32[2,128]{1,0:T(2,128)S(1)}, f32[16,40,128]{2,1,0:T(8,128)S(1)}, f32[1,128]{1,0:T(1,128)S(1)}) custom-call(bf16[8,768]{1,0:T(8,128)(2,1)S(1)} %copy-done.4, bf16[768,512]{1,0:T(8,128)(2,1)S(1)} %copy-done.1, bf16[512,512]{1,0:T(8,128)(2,1)S(1)} %copy-done.2, bf16[1387,512]{1,0:T(8,128)(2,1)S(1)} %copy-done, s32[2,128]{1,0:T(2,128)S(1)} %copy-done.6, ...), custom_call_target="tpu_custom_call" | custom-call | tf_op jit(solution)/shard_map/step/pallas_call | solution.py:509
  80.7 0.0 copy-start.3
  80.7 0.7 copy-done.3
  81.4 0.5 copy-done.10
  81.9 0.6 copy-done.11
  82.5 1.7 %finish.1 = (f32[2,128]{1,0:T(2,128)}, f32[96,512]{1,0:T(8,128)}, f32[64,512]{1,0:T(8,128)}) custom-call(f32[2,128]{1,0:T(2,128)} %copy-done.10, f32[16,40,128]{2,1,0:T(8,128)} %copy-done.3, f32[1,128]{1,0:T(1,128)} %copy-done.11), custom_call_target="tpu_custom_call" | custom-call | tf_op jit(solution)/shard_map/finish/pallas_call | solution.py:574
  (2 shorter events, 0.0 us)
Async XLA Ops:
  0.6 1.4 %copy-start = (bf16[1387,512]{1,0:T(8,128)(2,1)S(1)}, bf16[1387,512]{1,0:T(8,128)(2,1)}, u32[]{:S(2)}) copy-start(bf16[1387,512]{1,0:T(8,128)(2,1)} %table_hbm.1) | copy-start | bytes 4260868
  2.0 1.1 %copy-start.1 = (bf16[768,512]{1,0:T(8,128)(2,1)S(1)}, bf16[768,512]{1,0:T(8,128)(2,1)}, u32[]{:S(2)}) copy-start(bf16[768,512]{1,0:T(8,128)(2,1)} %w1_hbm.1) | copy-start | bytes 2359300
  3.1 1.0 %copy-start.2 = (bf16[512,512]{1,0:T(8,128)(2,1)S(1)}, bf16[512,512]{1,0:T(8,128)(2,1)}, u32[]{:S(2)}) copy-start(bf16[512,512]{1,0:T(8,128)(2,1)} %w2_hbm.1) | copy-start | bytes 1572868
  4.2 0.7 copy-start.4
  4.9 0.7 copy-start.5
  5.6 0.7 copy-start.6
  6.2 0.7 copy-start.7
  6.9 0.7 copy-start.8
  7.6 0.7 copy-start.9
  80.7 0.7 copy-start.3
  81.4 0.5 copy-start.10
  81.9 0.6 copy-start.11

commit v3 on v2

--- a/solution.py
+++ b/solution.py
@@ -12,6 +12,8 @@
 BF = jnp.bfloat16
 F32 = jnp.float32
 HOP = 3
+NEAR = 4
+RELAY = {0: (4, 2, 1), 2: (1,), 4: (4, 2, 1), 6: (1,)}
 
 
 def mm(a, b):
@@ -85,6 +87,7 @@
     squares,
     load_sem,
     send_sem,
+    line_sem,
     sem_y,
     sem_x,
     sem_z,
@@ -97,6 +100,7 @@
     sem_p,
     sem_c,
     sem_s,
+    sem_t,
 ):
     nzh, na, ng = dims
     nz = nzh * ng
@@ -124,23 +128,29 @@
         return dev(div(to, ng), x, y, c, rem(to, ng))
 
     other_core = dev(zh, x, y, 1 - c, g)
-    pending = []
-    counter = [0]
-
-    def push(src, dst, sem, target, keep=True):
-        copy = pltpu.make_async_remote_copy(
+    conditional = []
+    sent = {}
+
+    def push(src, dst, sem, target, group):
+        sent[group] = sent.get(group, 0) + 1
+        pltpu.make_async_remote_copy(
             src_ref=src,
             dst_ref=dst,
-            send_sem=send_sem.at[counter[0]],
+            send_sem=send_sem.at[group],
             recv_sem=sem,
             device_id=target,
             device_id_type=MESH,
-        )
-        counter[0] += 1
-        copy.start()
-        if keep:
-            pending.append(copy)
-        return copy
+        ).start()
+
+    def all_sent(group, like):
+        pltpu.make_async_remote_copy(
+            src_ref=like,
+            dst_ref=like,
+            send_sem=send_sem.at[group],
+            recv_sem=sem_core.at[0],
+            device_id=other_core,
+            device_id_type=MESH,
+        ).wait_send()
 
     def arrived(dst, sem):
         pltpu.make_async_remote_copy(
@@ -152,32 +162,88 @@
             device_id_type=MESH,
         ).wait_recv()
 
-    def ring(buf, sem):
-        reach = {1: nz // 2, -1: nz - 1 - nz // 2}
-        seen = set()
-        for base in range(0, reach[1], HOP):
-            for way in (1, -1):
-                if base >= reach[way]:
+    def ring(buf, sem, group):
+        pieces = [(r, way) for r in range(2) for way in ((1, -1) if r == 0 else (-1, 1))]
+
+        def last(r, way):
+            return nz // 2 if (way == 1) == (r == 0) else nz // 2 - 1
+
+        waited = set()
+        for base in sorted(RELAY):
+            for r, way in pieces:
+                if base > last(r, way):
                     continue
                 source = rem(z - way * base + nz, nz)
+                held, flag = buf.at[source, r], sem.at[source, r]
                 if base:
-                    arrived(buf.at[source], sem.at[source])
+                    arrived(held, flag)
+                    waited.add((r, way, base))
+                for step in RELAY[base]:
+                    if base + step <= last(r, way):
+                        push(held, held, flag, on_ring(way * step), group)
+            yield
+        for r, way in pieces:
+            for dist in range(1, last(r, way) + 1):
+                if (r, way, dist) not in waited:
+                    source = rem(z - way * dist + nz, nz)
+                    arrived(buf.at[source, r], sem.at[source, r])
+
+    def push_if(cond, *what):
+        index = len(conditional)
+
+        def make():
+            src, dst, sem, target = what
+            return pltpu.make_async_remote_copy(
+                src_ref=src,
+                dst_ref=dst,
+                send_sem=line_sem.at[index],
+                recv_sem=sem,
+                device_id=target,
+                device_id_type=MESH,
+            )
+
+        @pl.when(cond)
+        def _():
+            make().start()
+
+        conditional.append((cond, make))
+
+    def arrived_if(cond, *what):
+        @pl.when(cond)
+        def _():
+            arrived(*what)
+
+    def line(buf, sem):
+        def within(k):
+            return jnp.logical_and(k >= 0, k < ng)
+
+        seen = set()
+        for base in range(0, ng - 1, HOP):
+            for way in (1, -1):
+                source = g - way * base
+                there = within(source)
+                held = buf.at[rem(source + ng, ng)]
+                flag = sem.at[rem(source + ng, ng)]
+                if base:
+                    arrived_if(there, held, flag)
                     seen.add(-way * base)
-                for step in range(min(HOP, reach[way] - base), 0, -1):
-                    push(buf.at[source], buf.at[source], sem.at[source], on_ring(way * step))
+                for step in range(min(HOP, ng - 1 - base), 0, -1):
+                    to = g + way * step
+                    both = jnp.logical_and(there, within(to))
+                    push_if(both, held, held, flag, dev(zh, x, y, c, rem(to + ng, ng)))
             yield
         for way in (1, -1):
-            for dist in range(1, reach[way] + 1):
+            for dist in range(1, ng):
                 if -way * dist not in seen:
-                    source = rem(z - way * dist + nz, nz)
-                    arrived(buf.at[source], sem.at[source])
+                    source = rem(g - way * dist + ng, ng)
+                    arrived_if(within(g - way * dist), buf.at[source], sem.at[source])
 
     barrier = pltpu.get_barrier_semaphore()
     peers = [
         dev(zh, x, xor(y, k >> 1), rem(c + (k & 1), 2), g) for k in range(1, 2 * na)
     ]
     peers += [dev(zh, xor(x, k), y, c, g) for k in range(1, na)]
-    near = min(HOP, nz // 2)
+    near = min(NEAR, nz // 2)
     peers += [on_ring(k) for k in range(1, nz) if min(k, nz - k) <= near]
     for peer in peers:
         pl.semaphore_signal(barrier, inc=1, device_id=peer, device_id_type=MESH)
@@ -185,7 +251,7 @@
     pairs = (
         (feat_hbm, feat),
         (feat_hbm, buf_y.at[0]),
-        (feat_hbm, buf_o.at[z]),
+        (feat_hbm, buf_o.at[g]),
         (partner_hbm, partner),
         (heads_hbm, heads),
         (rels_hbm, rels),
@@ -204,8 +270,9 @@
     pl.semaphore_wait(barrier, len(peers))
 
     for k in range(1, 2 * na):
-        push(feat, buf_y.at[k], sem_y.at[k], dev(zh, x, xor(y, k >> 1), rem(c + (k & 1), 2), g))
-    own_ring = ring(buf_o, sem_o)
+        target = dev(zh, x, xor(y, k >> 1), rem(c + (k & 1), 2), g)
+        push(feat, buf_y.at[k], sem_y.at[0], target, 0)
+    own_ring = line(buf_o, sem_o)
     next(own_ring)
 
     for load in loads[3:9]:
@@ -222,20 +289,18 @@
         rel_rows[r] = mm(pick.astype(BF), table[...]).astype(BF)
 
     masks = [partner[r, 0] for r in range(2)]
-    for k in range(1, 2 * na):
-        arrived(buf_y.at[k], sem_y.at[k])
+    arrived(buf_y.at[pl.ds(1, 2 * na - 1)], sem_y.at[0])
     for r in range(2):
         send_x[r] = buf_y[masks[r] % (2 * na)]
     for k in range(1, na):
-        push(send_x, buf_x.at[k], sem_x.at[k], dev(zh, xor(x, k), y, c, g))
+        push(send_x, buf_x.at[k], sem_x.at[0], dev(zh, xor(x, k), y, c, g), 1)
     next(own_ring, None)
     buf_x[0] = send_x[...]
-    for k in range(1, na):
-        arrived(buf_x.at[k], sem_x.at[k])
+    arrived(buf_x.at[pl.ds(1, na - 1)], sem_x.at[0])
     for r in range(2):
         buf_z[z, r] = buf_x[(masks[r] // (2 * na)) % na, r]
 
-    far_ring = ring(buf_z, sem_z)
+    far_ring = ring(buf_z, sem_z, 2)
     next(far_ring)
     for _ in own_ring:
         pass
@@ -255,7 +320,7 @@
         xt[:, at : at + count] = jnp.transpose(x_rows)
         ht[:, at : at + count] = jnp.transpose(hidden)
 
-    own_x = buf_o[pl.ds(zh * ng, ng)].astype(F32).reshape(rows, feat.shape[1]).astype(BF)
+    own_x = buf_o[...].astype(F32).reshape(rows, feat.shape[1]).astype(BF)
     encode(own_x, 2 * rows, rows, 2 * rows)
     picks = []
     for r in range(2):
@@ -331,7 +396,7 @@
             core_send[gh, i, part_w2:block] = high.astype(BF)
 
         slice_of(2 * gh + 1 - c, put_send)
-        push(core_send.at[gh], core_recv.at[gh], sem_core.at[gh], other_core)
+        push(core_send.at[gh], core_recv.at[gh], sem_core.at[gh], other_core, 3)
     for gh in range(halves):
 
         def put_own(i, low, high, gh=gh):
@@ -359,125 +424,96 @@
         send_1[gh] = total[gh].astype(BF)
         for j in range(1, na):
             k = rem(a + j, na)
-            push(send_1.at[gh, k], recv_1.at[a, gh], sem_1.at[a, gh], along_a(k))
+            push(send_1.at[gh, k], recv_1.at[gh, a], sem_1.at[gh], along_a(k), 4)
     for gh in range(halves):
         part = total[gh, a]
+        arrived(recv_1.at[gh, pl.ds(0, na - 1)], sem_1.at[gh])
         for j in range(1, na):
-            k = rem(a + j, na)
-            arrived(recv_1.at[k, gh], sem_1.at[k, gh])
-            part = part + recv_1[k, gh].astype(F32)
+            part = part + recv_1[gh, rem(a + j, na)].astype(F32)
         for i in range(na):
-            part_2[i, gh] = part[:, i * width : (i + 1) * width]
-            send_2[i, gh] = part[:, i * width : (i + 1) * width].astype(BF)
-    for j in range(1, na):
-        k = rem(b + j, na)
-        push(send_2.at[k], recv_2.at[b], sem_2.at[b], along_b(k))
-    part = part_2[b]
-    for j in range(1, na):
-        k = rem(b + j, na)
-        arrived(recv_2.at[k], sem_2.at[k])
-        part = part + recv_2[k].astype(F32)
-    send_z[...] = part.astype(BF)
-
+            part_2[gh, i] = part[:, i * width : (i + 1) * width]
+            send_2[gh, i] = part[:, i * width : (i + 1) * width].astype(BF)
+        for j in range(1, na):
+            k = rem(b + j, na)
+            push(send_2.at[gh, k], recv_2.at[gh, b], sem_2.at[gh], along_b(k), 5)
     matched = rem(g + c, 2) == 0
-    conditional = []
     for gh in range(halves):
+        part = part_2[gh, b]
+        arrived(recv_2.at[gh, pl.ds(0, na - 1)], sem_2.at[gh])
+        for j in range(1, na):
+            part = part + recv_2[gh, rem(b + j, na)].astype(F32)
+        send_z[gh] = part.astype(BF)
+        to = 2 * gh + c
         for zp in range(nzh):
-            to = 2 * gh + c
-            elsewhere = jnp.logical_or(rem(zh + zp, nzh) != zh, to != g)
-            conditional.append((elsewhere, gh, zp, counter[0]))
+            to_z = rem(zh + zp, nzh)
+            elsewhere = jnp.logical_or(to_z != zh, to != g)
+            target = dev(to_z, x, y, c, to)
 
             @pl.when(elsewhere)
-            def _(gh=gh, zp=zp, to=to):
-                push(
-                    send_z.at[gh],
-                    recv_z.at[z],
-                    sem_rz.at[z],
-                    dev(rem(zh + zp, nzh), x, y, c, to),
-                    keep=False,
-                )
+            def _(gh=gh, target=target):
+                push(send_z.at[gh], recv_z.at[z], sem_rz.at[0], target, 6)
+
 
     @pl.when(matched)
     def _():
         recv_z[z] = send_z[div(g, 2)]
-        for k in range(1, nz):
-            source = rem(z + k, nz)
-            arrived(recv_z.at[source], sem_rz.at[source])
+        arrived(recv_z.at[pl.ds(0, nz - 1)], sem_rz.at[0])
         piece = jnp.zeros((block, width), F32)
         for k in range(nz):
             piece = piece + recv_z[k].astype(F32)
         slot = a * na + b
         places = na * na
         parts_sq[slot] = jnp.full((1, width), jnp.sum(piece * piece), F32)
-        mine = []
         for t in range(1, places):
-            to = rem(slot + t, places)
-            mine.append(
-                push(parts_sq.at[slot], parts_sq.at[slot], sem_q.at[slot], in_plane(to), keep=False)
-            )
+            to = in_plane(rem(slot + t, places))
+            push(parts_sq.at[slot], parts_sq.at[slot], sem_q.at[0], to, 7)
         gathered[slot] = piece
         for t in range(1, places):
-            to = rem(slot + t, places)
-            mine.append(
-                push(gathered.at[slot], gathered.at[slot], sem_p.at[slot], in_plane(to), keep=False)
-            )
-        mine.append(push(gathered.at[slot], gathered.at[slot], sem_c.at[slot], other_core, keep=False))
-        for t in range(1, places):
-            source = rem(slot + t, places)
-            arrived(parts_sq.at[source], sem_q.at[source])
+            to = in_plane(rem(slot + t, places))
+            push(gathered.at[slot], gathered.at[slot], sem_p.at[0], to, 8)
+        arrived(parts_sq.at[pl.ds(0, places - 1)], sem_q.at[0])
         ss = parts_sq[0]
         for i in range(1, places):
             ss = ss + parts_sq[i]
         squares[g] = ss
-        for k in range(ng - 1, 0, -1):
-            for cc in range(2):
-                mine.append(
-                    push(
-                        squares.at[g],
-                        squares.at[g],
-                        sem_s.at[g],
-                        dev(zh, x, y, cc, rem(g + k, ng)),
-                        keep=False,
-                    )
-                )
-        mine.append(push(squares.at[g], squares.at[g], sem_s.at[g], other_core, keep=False))
-        for t in range(places - 1, 0, -1):
-            source = rem(slot + t, places)
-            arrived(gathered.at[source], sem_p.at[source])
-            mine.append(
-                push(gathered.at[source], gathered.at[source], sem_c.at[source], other_core, keep=False)
-            )
-        for copy in mine:
-            copy.wait_send()
+        for k in sorted(range(1 - ng // 2, ng // 2 + 1), key=abs, reverse=True):
+            if k:
+                to = rem(z + k + nz, nz)
+                for cc in range(2):
+                    target = dev(div(to, ng), x, y, cc, rem(to, ng))
+                    push(squares.at[g], squares.at[g], sem_s.at[0], target, 9)
+        push(squares.at[g], squares.at[g], sem_t.at[0], other_core, 9)
+        arrived(gathered.at[pl.ds(0, places - 1)], sem_p.at[0])
+        push(gathered, gathered, sem_c.at[0], other_core, 10)
+        all_sent(7, parts_sq.at[pl.ds(0, places - 1)])
+        all_sent(8, gathered.at[pl.ds(0, places - 1)])
+        all_sent(9, parts_sq.at[pl.ds(0, 2 * ng - 1)])
+        all_sent(10, gathered)
+        all_sent(6, recv_z.at[pl.ds(0, halves * nzh - 1)])
 
     @pl.when(jnp.logical_not(matched))
     def _():
-        arrived(squares.at[g], sem_s.at[g])
-        for k in range(na * na):
-            arrived(gathered.at[k], sem_c.at[k])
-
-    for k in range(1, ng):
-        source = rem(g + k, ng)
-        arrived(squares.at[source], sem_s.at[source])
+        arrived(squares.at[g], sem_t.at[0])
+        arrived(gathered, sem_c.at[0])
+        all_sent(6, recv_z.at[pl.ds(0, halves * nzh)])
+
+    arrived(squares.at[pl.ds(0, ng - 1)], sem_s.at[0])
     ss = squares[0]
     for k in range(1, ng):
         ss = ss + squares[k]
     norm_out[...] = ss
 
-    for copy in pending:
-        copy.wait_send()
-    for elsewhere, gh, zp, index in conditional:
-
-        @pl.when(elsewhere)
-        def _(gh=gh, zp=zp, index=index):
-            pltpu.make_async_remote_copy(
-                src_ref=send_z.at[gh],
-                dst_ref=recv_z.at[z],
-                send_sem=send_sem.at[index],
-                recv_sem=sem_rz.at[z],
-                device_id=dev(rem(zh + zp, nzh), x, y, c, 2 * gh + c),
-                device_id_type=MESH,
-            ).wait_send()
+    all_sent(0, buf_y.at[pl.ds(1, 2 * na - 1)])
+    all_sent(1, buf_x.at[pl.ds(1, na - 1)])
+    all_sent(2, buf_z.at[pl.ds(0, nz - 1)])
+    all_sent(3, core_send)
+    all_sent(4, send_1.at[pl.ds(0, halves), pl.ds(0, na - 1)])
+    all_sent(5, send_2.at[pl.ds(0, halves), pl.ds(0, na - 1)])
+    for cond, make in conditional:
+
+        @pl.when(cond)
+        def _(make=make):
+            make().wait_send()
 
 
 def finish(na, count, loss_in, pieces, squares, loss_out, g1_out, g2_out):
@@ -530,7 +566,7 @@
             V((2, own, d_in), BF),
             V((na, 2, own, d_in), BF),
             V((nz, 2, own, d_in), BF),
-            V((nz, own, d_in), BF),
+            V((ng, own, d_in), BF),
             V((2, edges, d_enc), BF),
             V((2, edges, d_enc), BF),
             V((3 * rows, d_enc), BF),
@@ -543,31 +579,33 @@
             V((halves, na, block, d_enc), BF),
             V((halves, na, block, d_enc), F32),
             V((halves, na, block, d_enc), BF),
-            V((na, halves, block, d_enc), BF),
-            V((na, halves, block, width), F32),
-            V((na, halves, block, width), BF),
-            V((na, halves, block, width), BF),
+            V((halves, na, block, d_enc), BF),
+            V((halves, na, block, width), F32),
+            V((halves, na, block, width), BF),
+            V((halves, na, block, width), BF),
             V((halves, block, width), BF),
             V((nz, block, width), BF),
             V((na * na, 1, width), F32),
             V((ng, 1, width), F32),
             S((11,)),
-            S((160,)),
-            S((2 * na,)),
-            S((na,)),
-            S((nz,)),
-            S((nz,)),
+            S((11,)),
+            S((14,)),
+            S((1,)),
+            S((1,)),
+            S((nz, 2)),
+            S((ng,)),
             S((halves,)),
-            S((na, halves)),
-            S((na,)),
-            S((nz,)),
-            S((na * na,)),
-            S((na * na,)),
-            S((na * na,)),
-            S((ng,)),
+            S((halves,)),
+            S((halves,)),
+            S((1,)),
+            S((1,)),
+            S((1,)),
+            S((1,)),
+            S((1,)),
+            S((1,)),
         ],
         compiler_params=pltpu.CompilerParams(
-            collective_id=0, has_side_effects=True, vmem_limit_bytes=24 * 1024 * 1024
+            collective_id=0, has_side_effects=True, vmem_limit_bytes=60 * 1024 * 1024
         ),
         name="step",
     )(features, w_first, w_second, table, heads, relations, tails, negatives, partner)

time: 84.6 us -> 69.9 us (0.83)
  local copies, waits for them, and re-layouts: 9.47 us -> 0 us
  Pallas kernels: 74.1 us -> 69.1 us
    unnamed x24 -> x0, local copies, waits for them, and re-layouts: 9.47 us -> none
    pallas_call x1, Pallas kernels: 72.4 us -> 67.4 us  [per_device(): pl.pallas_call(functools.partial(body, dims), out_shape=(jax.ShapeDtypeSt...]
where the time goes in v3:
time: 69.9 us; the launch traced here: 69.7 us
  Pallas kernels  69.1 us (99%)
    pallas_call x1, Pallas kernels, per_device(): pl.pallas_call(functools.partial(body, dims), out_shape=(jax.ShapeDtypeSt...  67.4 us
    pallas_call x1, Pallas kernels, per_device(): pl.pallas_call(functools.partial(finish, na, float(w_first.size + w_secon...  1.73 us

profile of v3, /device:TPU:1, one launch (start us, length us, event | category | flops | bytes accessed | tf_op | source)
XLA Modules:
  0.0 69.7 jit_solution(7907436049078809866)
XLA Ops:
  0.6 67.4 %step.1 = (f32[2,128]{1,0:T(2,128)}, f32[16,40,128]{2,1,0:T(8,128)}, f32[1,128]{1,0:T(1,128)}) custom-call(bf16[8,768]{1,0:T(8,128)(2,1)} %feat_hbm.1, bf16[768,512]{1,0:T(8,128)(2,1)} %w1_hbm.1, bf16[512,512]{1,0:T(8,128)(2,1)} %w2_hbm.1, bf16[1387,512]{1,0:T(8,128)(2,1)} %table_hbm.1, s32[2,128]{1,0:T(2,128)} %heads_hbm.1, s32[2,128]{1,0:T(2,128)} %rels_hbm.1, ...), custom_call_target="tpu_custom_call" | custom-call | tf_op jit(solution)/shard_map/step/pallas_call | solution.py:545
  68.0 1.7 %finish.1 = (f32[2,128]{1,0:T(2,128)}, f32[96,512]{1,0:T(8,128)}, f32[64,512]{1,0:T(8,128)}) custom-call(f32[2,128]{1,0:T(2,128)} %get-tuple-element.6.loss_in, f32[16,40,128]{2,1,0:T(8,128)} %get-tuple-element.7.pieces, f32[1,128]{1,0:T(1,128)} %get-tuple-element.8.squares), custom_call_target="tpu_custom_call" | custom-call | tf_op jit(solution)/shard_map/finish/pallas_call | solution.py:612

commit v4 on v3

--- a/solution.py
+++ b/solution.py
@@ -13,7 +13,8 @@
 F32 = jnp.float32
 HOP = 3
 NEAR = 4
-RELAY = {0: (4, 2, 1), 2: (1,), 4: (4, 2, 1), 6: (1,)}
+STEP = 1
+RELAY = {0: (4, 3, 2, 1), 4: (4, 3, 2, 1)}
 
 
 def mm(a, b):
@@ -61,8 +62,6 @@
     partner,
     ids,
     buf_y,
-    send_x,
-    buf_x,
     buf_z,
     buf_o,
     rel_rows,
@@ -75,26 +74,21 @@
     ht,
     core_send,
     core_recv,
-    total,
     send_1,
     recv_1,
-    part_2,
-    send_2,
-    recv_2,
     send_z,
     recv_z,
     parts_sq,
     squares,
+    spare,
     load_sem,
     send_sem,
     line_sem,
     sem_y,
-    sem_x,
     sem_z,
     sem_o,
     sem_core,
     sem_1,
-    sem_2,
     sem_rz,
     sem_q,
     sem_p,
@@ -163,30 +157,26 @@
         ).wait_recv()
 
     def ring(buf, sem, group):
-        pieces = [(r, way) for r in range(2) for way in ((1, -1) if r == 0 else (-1, 1))]
-
-        def last(r, way):
-            return nz // 2 if (way == 1) == (r == 0) else nz // 2 - 1
-
+        reach = {1: nz // 2, -1: nz - 1 - nz // 2}
         waited = set()
         for base in sorted(RELAY):
-            for r, way in pieces:
-                if base > last(r, way):
+            for way in (1, -1):
+                if base > reach[way]:
                     continue
                 source = rem(z - way * base + nz, nz)
-                held, flag = buf.at[source, r], sem.at[source, r]
+                held, flag = buf.at[source], sem.at[source]
                 if base:
                     arrived(held, flag)
-                    waited.add((r, way, base))
+                    waited.add(way * base)
                 for step in RELAY[base]:
-                    if base + step <= last(r, way):
+                    if base + step <= reach[way]:
                         push(held, held, flag, on_ring(way * step), group)
             yield
-        for r, way in pieces:
-            for dist in range(1, last(r, way) + 1):
-                if (r, way, dist) not in waited:
+        for way in (1, -1):
+            for dist in range(1, reach[way] + 1):
+                if way * dist not in waited:
                     source = rem(z - way * dist + nz, nz)
-                    arrived(buf.at[source, r], sem.at[source, r])
+                    arrived(buf.at[source], sem.at[source])
 
     def push_if(cond, *what):
         index = len(conditional)
@@ -239,10 +229,13 @@
                     arrived_if(within(g - way * dist), buf.at[source], sem.at[source])
 
     barrier = pltpu.get_barrier_semaphore()
-    peers = [
-        dev(zh, x, xor(y, k >> 1), rem(c + (k & 1), 2), g) for k in range(1, 2 * na)
-    ]
-    peers += [dev(zh, xor(x, k), y, c, g) for k in range(1, na)]
+    places = na * na
+    shifts = sorted(range(1, 2 * places), key=lambda k: -sum(min(v, na - v) for v in (k // (2 * na), k // 2 % na)))
+
+    def shifted(k):
+        return dev(zh, xor(x, k // (2 * na)), xor(y, k // 2 % na), rem(c + k % 2, 2), g)
+
+    peers = [shifted(k) for k in shifts]
     near = min(NEAR, nz // 2)
     peers += [on_ring(k) for k in range(1, nz) if min(k, nz - k) <= near]
     for peer in peers:
@@ -269,9 +262,8 @@
         load.wait()
     pl.semaphore_wait(barrier, len(peers))
 
-    for k in range(1, 2 * na):
-        target = dev(zh, x, xor(y, k >> 1), rem(c + (k & 1), 2), g)
-        push(feat, buf_y.at[k], sem_y.at[0], target, 0)
+    for k in shifts:
+        push(feat, buf_y.at[k], sem_y.at[0], shifted(k), 0)
     own_ring = line(buf_o, sem_o)
     next(own_ring)
 
@@ -289,17 +281,10 @@
         rel_rows[r] = mm(pick.astype(BF), table[...]).astype(BF)
 
     masks = [partner[r, 0] for r in range(2)]
-    arrived(buf_y.at[pl.ds(1, 2 * na - 1)], sem_y.at[0])
+    next(own_ring, None)
+    arrived(buf_y.at[pl.ds(1, 2 * places - 1)], sem_y.at[0])
     for r in range(2):
-        send_x[r] = buf_y[masks[r] % (2 * na)]
-    for k in range(1, na):
-        push(send_x, buf_x.at[k], sem_x.at[0], dev(zh, xor(x, k), y, c, g), 1)
-    next(own_ring, None)
-    buf_x[0] = send_x[...]
-    arrived(buf_x.at[pl.ds(1, na - 1)], sem_x.at[0])
-    for r in range(2):
-        buf_z[z, r] = buf_x[(masks[r] // (2 * na)) % na, r]
-
+        buf_z[z, r] = buf_y[masks[r] % (2 * places)]
     far_ring = ring(buf_z, sem_z, 2)
     next(far_ring)
     for _ in own_ring:
@@ -342,7 +327,7 @@
 
     far = []
     for r in range(2):
-        half_of = rem(zh + (masks[r] // (2 * na * na)) % 2, 2)
+        half_of = rem(zh + (masks[r] // (2 * places)) % 2, 2)
         rows_r = buf_z[pl.ds(half_of * ng, ng), r]
         far.append(rows_r.astype(F32).reshape(rows, feat.shape[1]))
     encode(jnp.concatenate(far, axis=0).astype(BF), 0, 2 * rows, 0)
@@ -397,51 +382,43 @@
 
         slice_of(2 * gh + 1 - c, put_send)
         push(core_send.at[gh], core_recv.at[gh], sem_core.at[gh], other_core, 3)
-    for gh in range(halves):
-
-        def put_own(i, low, high, gh=gh):
-            total[gh, i, 0:part_w2] = low
-            total[gh, i, part_w2:block] = high
-
-        slice_of(2 * gh + c, put_own)
-
     a = c * x + (1 - c) * y
     b = c * y + (1 - c) * x
-
-    def along_a(k):
-        return dev(zh, c * k + (1 - c) * x, c * y + (1 - c) * k, c, g)
+    slot = a * na + b
+    ways = sorted(range(1, places), key=lambda k: -sum(min(v, na - v) for v in (k // na, k % na)))
 
     def in_plane(k):
         ka, kb = div(k, na), rem(k, na)
         return dev(zh, c * ka + (1 - c) * kb, c * kb + (1 - c) * ka, c, g)
 
-    def along_b(k):
-        return dev(zh, c * x + (1 - c) * k, c * k + (1 - c) * y, c, g)
-
-    for gh in range(halves):
-        arrived(core_recv.at[gh], sem_core.at[gh])
-        total[gh] = total[gh] + core_recv[gh].astype(F32)
-        send_1[gh] = total[gh].astype(BF)
-        for j in range(1, na):
-            k = rem(a + j, na)
-            push(send_1.at[gh, k], recv_1.at[gh, a], sem_1.at[gh], along_a(k), 4)
-    for gh in range(halves):
-        part = total[gh, a]
-        arrived(recv_1.at[gh, pl.ds(0, na - 1)], sem_1.at[gh])
-        for j in range(1, na):
-            part = part + recv_1[gh, rem(a + j, na)].astype(F32)
-        for i in range(na):
-            part_2[gh, i] = part[:, i * width : (i + 1) * width]
-            send_2[gh, i] = part[:, i * width : (i + 1) * width].astype(BF)
-        for j in range(1, na):
-            k = rem(b + j, na)
-            push(send_2.at[gh, k], recv_2.at[gh, b], sem_2.at[gh], along_b(k), 5)
+    def turned(k):
+        return rem(a + k // na, na) * na + rem(b + k % na, na)
+
+    for first in range(0, halves, STEP):
+        for gh in range(first, min(first + STEP, halves)):
+            local = []
+            slice_of(2 * gh + c, lambda i, low, high: local.append((low, high)))
+            arrived(core_recv.at[gh], sem_core.at[gh])
+            for i, (low, high) in enumerate(local):
+                low = (low + core_recv[gh, i, 0:part_w2].astype(F32)).astype(BF)
+                high = (high + core_recv[gh, i, part_w2:block].astype(F32)).astype(BF)
+                for k in range(na):
+                    column = slice(k * width, (k + 1) * width)
+                    send_1[i * na + k, gh, 0:part_w2] = low[:, column]
+                    send_1[i * na + k, gh, part_w2:block] = high[:, column]
+        some = pl.ds(first, min(STEP, halves - first))
+        for k in ways:
+            to = turned(k)
+            push(send_1.at[to, some], recv_1.at[slot, some], sem_1.at[first], in_plane(to), 4)
+        recv_1[slot, some] = send_1[slot, some]
     matched = rem(g + c, 2) == 0
     for gh in range(halves):
-        part = part_2[gh, b]
-        arrived(recv_2.at[gh, pl.ds(0, na - 1)], sem_2.at[gh])
-        for j in range(1, na):
-            part = part + recv_2[gh, rem(b + j, na)].astype(F32)
+        if gh % STEP == 0:
+            some = pl.ds(gh, min(STEP, halves - gh))
+            arrived(recv_1.at[pl.ds(0, places - 1), some], sem_1.at[gh])
+        part = recv_1[0, gh].astype(F32)
+        for k in range(1, places):
+            part = part + recv_1[k, gh].astype(F32)
         send_z[gh] = part.astype(BF)
         to = 2 * gh + c
         for zp in range(nzh):
@@ -461,54 +438,51 @@
         piece = jnp.zeros((block, width), F32)
         for k in range(nz):
             piece = piece + recv_z[k].astype(F32)
-        slot = a * na + b
-        places = na * na
-        parts_sq[slot] = jnp.full((1, width), jnp.sum(piece * piece), F32)
-        for t in range(1, places):
-            to = in_plane(rem(slot + t, places))
-            push(parts_sq.at[slot], parts_sq.at[slot], sem_q.at[0], to, 7)
-        gathered[slot] = piece
-        for t in range(1, places):
-            to = in_plane(rem(slot + t, places))
-            push(gathered.at[slot], gathered.at[slot], sem_p.at[0], to, 8)
-        arrived(parts_sq.at[pl.ds(0, places - 1)], sem_q.at[0])
-        ss = parts_sq[0]
-        for i in range(1, places):
-            ss = ss + parts_sq[i]
-        squares[g] = ss
+        squares[g] = jnp.full((1, width), jnp.sum(piece * piece), F32)
         for k in sorted(range(1 - ng // 2, ng // 2 + 1), key=abs, reverse=True):
             if k:
                 to = rem(z + k + nz, nz)
-                for cc in range(2):
-                    target = dev(div(to, ng), x, y, cc, rem(to, ng))
-                    push(squares.at[g], squares.at[g], sem_s.at[0], target, 9)
-        push(squares.at[g], squares.at[g], sem_t.at[0], other_core, 9)
+                target = dev(div(to, ng), x, y, rem(c + k + nz, 2), rem(to, ng))
+                push(squares.at[g], squares.at[g], sem_s.at[0], target, 7)
+        gathered[slot] = piece.astype(BF)
+        for k in ways:
+            push(gathered.at[slot], gathered.at[slot], sem_p.at[0], in_plane(turned(k)), 8)
+        arrived(squares.at[pl.ds(0, ng - 1)], sem_s.at[0])
+        ss = squares[0]
+        for k in range(1, ng):
+            ss = ss + squares[k]
+        parts_sq[slot] = ss
+        for k in ways:
+            for cc in range(2):
+                ka, kb = div(turned(k), na), rem(turned(k), na)
+                target = dev(zh, c * ka + (1 - c) * kb, c * kb + (1 - c) * ka, cc, g)
+                push(parts_sq.at[slot], parts_sq.at[slot], sem_q.at[0], target, 9)
+        push(parts_sq.at[slot], parts_sq.at[slot], sem_t.at[0], other_core, 10)
         arrived(gathered.at[pl.ds(0, places - 1)], sem_p.at[0])
-        push(gathered, gathered, sem_c.at[0], other_core, 10)
-        all_sent(7, parts_sq.at[pl.ds(0, places - 1)])
+        push(gathered, gathered, sem_c.at[0], other_core, 11)
+        all_sent(7, squares.at[pl.ds(0, ng - 1)])
         all_sent(8, gathered.at[pl.ds(0, places - 1)])
-        all_sent(9, parts_sq.at[pl.ds(0, 2 * ng - 1)])
-        all_sent(10, gathered)
+        all_sent(9, spare)
+        all_sent(10, parts_sq.at[0])
+        all_sent(11, gathered)
         all_sent(6, recv_z.at[pl.ds(0, halves * nzh - 1)])
 
     @pl.when(jnp.logical_not(matched))
     def _():
-        arrived(squares.at[g], sem_t.at[0])
+        arrived(parts_sq.at[0], sem_t.at[0])
         arrived(gathered, sem_c.at[0])
         all_sent(6, recv_z.at[pl.ds(0, halves * nzh)])
 
-    arrived(squares.at[pl.ds(0, ng - 1)], sem_s.at[0])
-    ss = squares[0]
-    for k in range(1, ng):
-        ss = ss + squares[k]
+    arrived(parts_sq.at[pl.ds(0, places - 1)], sem_q.at[0])
+    ss = parts_sq[0]
+    for k in range(1, places):
+        ss = ss + parts_sq[k]
     norm_out[...] = ss
 
-    all_sent(0, buf_y.at[pl.ds(1, 2 * na - 1)])
-    all_sent(1, buf_x.at[pl.ds(1, na - 1)])
+    all_sent(0, buf_y.at[pl.ds(1, 2 * places - 1)])
     all_sent(2, buf_z.at[pl.ds(0, nz - 1)])
     all_sent(3, core_send)
-    all_sent(4, send_1.at[pl.ds(0, halves), pl.ds(0, na - 1)])
-    all_sent(5, send_2.at[pl.ds(0, halves), pl.ds(0, na - 1)])
+    all_sent(4, send_1.at[pl.ds(0, places - 1)])
     for cond, make in conditional:
 
         @pl.when(cond)
@@ -525,8 +499,8 @@
     for i in range(na):
         for k in range(na):
             column = slice(k * width, (k + 1) * width)
-            g2_out[i * low : (i + 1) * low, column] = pieces[i * na + k, 0:low] * factor
-            g1_out[i * high : (i + 1) * high, column] = pieces[i * na + k, low:] * factor
+            g2_out[i * low : (i + 1) * low, column] = pieces[i * na + k, 0:low].astype(F32) * factor
+            g1_out[i * high : (i + 1) * high, column] = pieces[i * na + k, low:].astype(F32) * factor
 
 
 def per_device(dims, features, w_first, w_second, table, heads, relations, tails, negatives, partner):
@@ -546,7 +520,7 @@
         functools.partial(body, dims),
         out_shape=(
             jax.ShapeDtypeStruct(heads.shape, F32),
-            jax.ShapeDtypeStruct((na * na, block, width), F32),
+            jax.ShapeDtypeStruct((na * na, block, width), BF),
             jax.ShapeDtypeStruct((1, width), F32),
         ),
         in_specs=[hbm] * 9,
@@ -562,9 +536,7 @@
             V(negatives.shape, jnp.int32),
             pltpu.SMEM(partner.shape, jnp.int32),
             V((8, edges), F32),
-            V((2 * na, own, d_in), BF),
-            V((2, own, d_in), BF),
-            V((na, 2, own, d_in), BF),
+            V((2 * na * na, own, d_in), BF),
             V((nz, 2, own, d_in), BF),
             V((ng, own, d_in), BF),
             V((2, edges, d_enc), BF),
@@ -577,24 +549,19 @@
             V((d_hid, lanes), BF),
             V((halves, na, block, d_enc), BF),
             V((halves, na, block, d_enc), BF),
-            V((halves, na, block, d_enc), F32),
-            V((halves, na, block, d_enc), BF),
-            V((halves, na, block, d_enc), BF),
-            V((halves, na, block, width), F32),
-            V((halves, na, block, width), BF),
-            V((halves, na, block, width), BF),
+            V((na * na, halves, block, width), BF),
+            V((na * na, halves, block, width), BF),
             V((halves, block, width), BF),
             V((nz, block, width), BF),
             V((na * na, 1, width), F32),
             V((ng, 1, width), F32),
+            V((2 * na * na - 2, 1, width), F32),
             S((11,)),
-            S((11,)),
+            S((12,)),
             S((14,)),
             S((1,)),
-            S((1,)),
-            S((nz, 2)),
+            S((nz,)),
             S((ng,)),
-            S((halves,)),
             S((halves,)),
             S((halves,)),
             S((1,)),

time: 69.9 us -> 68.9 us (0.986)
  Pallas kernels: 69.1 us -> 68.1 us
    pallas_call x1, Pallas kernels: 67.4 us -> 66.4 us  [per_device(): pl.pallas_call(functools.partial(body, dims), out_shape=(jax.ShapeDtypeSt...]
where the time goes in v4:
time: 68.9 us; the launch traced here: 68.7 us
  Pallas kernels  68.1 us (99%)
    pallas_call x1, Pallas kernels, per_device(): pl.pallas_call(functools.partial(body, dims), out_shape=(jax.ShapeDtypeSt...  66.4 us
    pallas_call x1, Pallas kernels, per_device(): pl.pallas_call(functools.partial(finish, na, float(w_first.size + w_secon...  1.67 us

profile of v4, /device:TPU:1, one launch (start us, length us, event | category | flops | bytes accessed | tf_op | source)
XLA Modules:
  0.0 68.7 jit_solution(5056045135211949884)
XLA Ops:
  0.6 66.4 %step.1 = (f32[2,128]{1,0:T(2,128)}, bf16[16,40,128]{2,1,0:T(8,128)(2,1)}, f32[1,128]{1,0:T(1,128)}) custom-call(bf16[8,768]{1,0:T(8,128)(2,1)} %feat_hbm.1, bf16[768,512]{1,0:T(8,128)(2,1)} %w1_hbm.1, bf16[512,512]{1,0:T(8,128)(2,1)} %w2_hbm.1, bf16[1387,512]{1,0:T(8,128)(2,1)} %table_hbm.1, s32[2,128]{1,0:T(2,128)} %heads_hbm.1, s32[2,128]{1,0:T(2,128)} %rels_hbm.1, ...), custom_call_target="tpu_custom_call" | custom-call | tf_op jit(solution)/shard_map/step/pallas_call | solution.py:519
  67.0 1.7 %finish.1 = (f32[2,128]{1,0:T(2,128)}, f32[96,512]{1,0:T(8,128)}, f32[64,512]{1,0:T(8,128)}) custom-call(f32[2,128]{1,0:T(2,128)} %get-tuple-element.6.loss_in, bf16[16,40,128]{2,1,0:T(8,128)(2,1)} %get-tuple-element.7.pieces, f32[1,128]{1,0:T(1,128)} %get-tuple-element.8.squares), custom_call_target="tpu_custom_call" | custom-call | tf_op jit(solution)/shard_map/finish/pallas_call | solution.py:579

commit v5 on v4

--- a/solution.py
+++ b/solution.py
@@ -11,7 +11,7 @@
 MESH = pl.DeviceIdType.MESH
 BF = jnp.bfloat16
 F32 = jnp.float32
-HOP = 3
+HOP = 4
 NEAR = 4
 STEP = 1
 RELAY = {0: (4, 3, 2, 1), 4: (4, 3, 2, 1)}
@@ -48,6 +48,9 @@
     tails_hbm,
     negs_hbm,
     partner_hbm,
+    loss_hbm,
+    pieces_hbm,
+    norm_hbm,
     loss_out,
     gathered,
     norm_out,
@@ -81,6 +84,7 @@
     parts_sq,
     squares,
     spare,
+    out_sem,
     load_sem,
     send_sem,
     line_sem,
@@ -157,11 +161,11 @@
         ).wait_recv()
 
     def ring(buf, sem, group):
-        reach = {1: nz // 2, -1: nz - 1 - nz // 2}
+        far = nz // 2
         waited = set()
         for base in sorted(RELAY):
             for way in (1, -1):
-                if base > reach[way]:
+                if base >= far:
                     continue
                 source = rem(z - way * base + nz, nz)
                 held, flag = buf.at[source], sem.at[source]
@@ -169,12 +173,15 @@
                     arrived(held, flag)
                     waited.add(way * base)
                 for step in RELAY[base]:
-                    if base + step <= reach[way]:
+                    if base + step < far:
                         push(held, held, flag, on_ring(way * step), group)
+                    elif base + step == far:
+                        part = held.at[(1 - way) // 2]
+                        push(part, part, flag, on_ring(way * step), group)
             yield
-        for way in (1, -1):
-            for dist in range(1, reach[way] + 1):
-                if way * dist not in waited:
+        for dist in range(1, far + 1):
+            for way in (1, -1):
+                if way * dist not in waited and (way == 1 or dist < far):
                     source = rem(z - way * dist + nz, nz)
                     arrived(buf.at[source], sem.at[source])
 
@@ -286,6 +293,7 @@
     for r in range(2):
         buf_z[z, r] = buf_y[masks[r] % (2 * places)]
     far_ring = ring(buf_z, sem_z, 2)
+    next(far_ring)
     next(far_ring)
     for _ in own_ring:
         pass
@@ -358,6 +366,12 @@
     wide = lax.broadcasted_iota(jnp.int32, (edges, 128), 1)
     both = jnp.where(wide == 0, losses[0], jnp.where(wide == 1, losses[1], 0.0))
     loss_out[...] = jnp.transpose(both)[0:2]
+    outs = [
+        pltpu.make_async_copy(loss_out, loss_hbm, out_sem.at[0]),
+        pltpu.make_async_copy(gathered, pieces_hbm, out_sem.at[1]),
+        pltpu.make_async_copy(norm_out, norm_hbm, out_sem.at[2]),
+    ]
+    outs[0].start()
 
     dpre[...] = (nt(grads[...], w2[...]) * slope[...]).astype(BF)
     rows_1, rows_2 = w1.shape[0] // ng, w2.shape[0] // ng
@@ -460,6 +474,7 @@
         push(parts_sq.at[slot], parts_sq.at[slot], sem_t.at[0], other_core, 10)
         arrived(gathered.at[pl.ds(0, places - 1)], sem_p.at[0])
         push(gathered, gathered, sem_c.at[0], other_core, 11)
+        outs[1].start()
         all_sent(7, squares.at[pl.ds(0, ng - 1)])
         all_sent(8, gathered.at[pl.ds(0, places - 1)])
         all_sent(9, spare)
@@ -471,6 +486,7 @@
     def _():
         arrived(parts_sq.at[0], sem_t.at[0])
         arrived(gathered, sem_c.at[0])
+        outs[1].start()
         all_sent(6, recv_z.at[pl.ds(0, halves * nzh)])
 
     arrived(parts_sq.at[pl.ds(0, places - 1)], sem_q.at[0])
@@ -478,6 +494,7 @@
     for k in range(1, places):
         ss = ss + parts_sq[k]
     norm_out[...] = ss
+    outs[2].start()
 
     all_sent(0, buf_y.at[pl.ds(1, 2 * places - 1)])
     all_sent(2, buf_z.at[pl.ds(0, nz - 1)])
@@ -489,18 +506,40 @@
         def _(make=make):
             make().wait_send()
 
-
-def finish(na, count, loss_in, pieces, squares, loss_out, g1_out, g2_out):
+    for copy in outs:
+        copy.wait()
+
+
+def finish(na, count, *refs):
+    loss_hbm, pieces_hbm, squares_hbm, loss_out, g1_hbm, g2_hbm = refs[:6]
+    pieces, squares, g1_out, g2_out, sem = refs[6:]
+    into = [
+        pltpu.make_async_copy(pieces_hbm, pieces, sem.at[0]),
+        pltpu.make_async_copy(squares_hbm, squares, sem.at[1]),
+        pltpu.make_async_copy(loss_hbm, loss_out, sem.at[2]),
+    ]
+    for copy in into:
+        copy.start()
     low = g2_out.shape[0] // na
     high = g1_out.shape[0] // na
     width = pieces.shape[2]
+    for copy in into[:2]:
+        copy.wait()
     factor = jnp.minimum(1.0, math.sqrt(count) / jnp.sqrt(squares[...] + 1e-06))
-    loss_out[...] = loss_in[...]
     for i in range(na):
         for k in range(na):
             column = slice(k * width, (k + 1) * width)
             g2_out[i * low : (i + 1) * low, column] = pieces[i * na + k, 0:low].astype(F32) * factor
             g1_out[i * high : (i + 1) * high, column] = pieces[i * na + k, low:].astype(F32) * factor
+    out = [
+        pltpu.make_async_copy(g1_out, g1_hbm, sem.at[3]),
+        pltpu.make_async_copy(g2_out, g2_hbm, sem.at[4]),
+    ]
+    for copy in out:
+        copy.start()
+    into[2].wait()
+    for copy in out:
+        copy.wait()
 
 
 def per_device(dims, features, w_first, w_second, table, heads, relations, tails, negatives, partner):
@@ -524,8 +563,11 @@
             jax.ShapeDtypeStruct((1, width), F32),
         ),
         in_specs=[hbm] * 9,
-        out_specs=(vmem, vmem, vmem),
+        out_specs=(hbm, hbm, hbm),
         scratch_shapes=[
+            V(heads.shape, F32),
+            V((na * na, block, width), BF),
+            V((1, width), F32),
             V(features.shape, BF),
             V(w_first.shape, BF),
             V(w_second.shape, BF),
@@ -556,6 +598,7 @@
             V((na * na, 1, width), F32),
             V((ng, 1, width), F32),
             V((2 * na * na - 2, 1, width), F32),
+            S((3,)),
             S((11,)),
             S((12,)),
             S((14,)),
@@ -583,8 +626,16 @@
             jax.ShapeDtypeStruct((rows_1, d_hid), F32),
             jax.ShapeDtypeStruct((rows_2, d_enc), F32),
         ),
-        in_specs=[vmem] * 3,
-        out_specs=(vmem, vmem, vmem),
+        in_specs=[hbm] * 3,
+        out_specs=(vmem, hbm, hbm),
+        scratch_shapes=[
+            V((na * na, block, width), BF),
+            V((1, width), F32),
+            V((rows_1, d_hid), F32),
+            V((rows_2, d_enc), F32),
+            S((5,)),
+        ],
+        compiler_params=pltpu.CompilerParams(vmem_limit_bytes=60 * 1024 * 1024),
         name="finish",
     )(loss, pieces, squares)
 

time: 68.9 us -> 67.7 us (0.983)
  Pallas kernels: 68.1 us -> 66.8 us
    pallas_call x1, Pallas kernels: 66.4 us -> 64.6 us  [per_device(): pl.pallas_call(functools.partial(body, dims), out_shape=(jax.ShapeDtypeSt...]
where the time goes in v5:
time: 67.7 us; the launch traced here: 67.5 us
  Pallas kernels  66.8 us (99%)
    pallas_call x1, Pallas kernels, per_device(): pl.pallas_call(functools.partial(body, dims), out_shape=(jax.ShapeDtypeSt...  64.6 us
    pallas_call x1, Pallas kernels, per_device(): pl.pallas_call(functools.partial(finish, na, float(w_first.size + w_secon...  2.27 us

profile of v5, /device:TPU:1, one launch (start us, length us, event | category | flops | bytes accessed | tf_op | source)
XLA Modules:
  0.0 67.5 jit_solution(12761733564509408976)
XLA Ops:
  0.6 64.6 %step.1 = (f32[2,128]{1,0:T(2,128)}, bf16[16,40,128]{2,1,0:T(8,128)(2,1)}, f32[1,128]{1,0:T(1,128)}) custom-call(bf16[8,768]{1,0:T(8,128)(2,1)} %feat_hbm.1, bf16[768,512]{1,0:T(8,128)(2,1)} %w1_hbm.1, bf16[512,512]{1,0:T(8,128)(2,1)} %w2_hbm.1, bf16[1387,512]{1,0:T(8,128)(2,1)} %table_hbm.1, s32[2,128]{1,0:T(2,128)} %heads_hbm.1, s32[2,128]{1,0:T(2,128)} %rels_hbm.1, ...), custom_call_target="tpu_custom_call" | custom-call | tf_op jit(solution)/shard_map/step/pallas_call | solution.py:558
  65.2 2.3 %finish.1 = (f32[2,128]{1,0:T(2,128)}, f32[96,512]{1,0:T(8,128)}, f32[64,512]{1,0:T(8,128)}) custom-call(f32[2,128]{1,0:T(2,128)} %get-tuple-element.6.refs_0_, bf16[16,40,128]{2,1,0:T(8,128)(2,1)} %get-tuple-element.7.refs_1_, f32[1,128]{1,0:T(1,128)} %get-tuple-element.8.refs_2_), custom_call_target="tpu_custom_call" | custom-call | tf_op jit(solution)/shard_map/finish/pallas_call | solution.py:622

commit v6 on v5

--- a/solution.py
+++ b/solution.py
@@ -13,7 +13,6 @@
 F32 = jnp.float32
 HOP = 4
 NEAR = 4
-STEP = 1
 RELAY = {0: (4, 3, 2, 1), 4: (4, 3, 2, 1)}
 
 
@@ -79,6 +78,8 @@
     core_recv,
     send_1,
     recv_1,
+    send_2,
+    recv_2,
     send_z,
     recv_z,
     parts_sq,
@@ -93,6 +94,7 @@
     sem_o,
     sem_core,
     sem_1,
+    sem_2,
     sem_rz,
     sem_q,
     sem_p,
@@ -408,31 +410,41 @@
     def turned(k):
         return rem(a + k // na, na) * na + rem(b + k % na, na)
 
-    for first in range(0, halves, STEP):
-        for gh in range(first, min(first + STEP, halves)):
-            local = []
-            slice_of(2 * gh + c, lambda i, low, high: local.append((low, high)))
-            arrived(core_recv.at[gh], sem_core.at[gh])
-            for i, (low, high) in enumerate(local):
-                low = (low + core_recv[gh, i, 0:part_w2].astype(F32)).astype(BF)
-                high = (high + core_recv[gh, i, part_w2:block].astype(F32)).astype(BF)
-                for k in range(na):
-                    column = slice(k * width, (k + 1) * width)
-                    send_1[i * na + k, gh, 0:part_w2] = low[:, column]
-                    send_1[i * na + k, gh, part_w2:block] = high[:, column]
-        some = pl.ds(first, min(STEP, halves - first))
-        for k in ways:
-            to = turned(k)
-            push(send_1.at[to, some], recv_1.at[slot, some], sem_1.at[first], in_plane(to), 4)
-        recv_1[slot, some] = send_1[slot, some]
+    def along_a(k):
+        return dev(zh, c * k + (1 - c) * x, c * y + (1 - c) * k, c, g)
+
+    def along_b(k):
+        return dev(zh, c * x + (1 - c) * k, c * k + (1 - c) * y, c, g)
+
+    steps = sorted(range(1, na), key=lambda k: -min(k, na - k))
+    for gh in range(halves):
+        local = []
+        slice_of(2 * gh + c, lambda i, low, high: local.append((low, high)))
+        arrived(core_recv.at[gh], sem_core.at[gh])
+        for i, (low, high) in enumerate(local):
+            low = low + core_recv[gh, i, 0:part_w2].astype(F32)
+            high = high + core_recv[gh, i, part_w2:block].astype(F32)
+            send_1[gh, i, 0:part_w2] = low.astype(BF)
+            send_1[gh, i, part_w2:block] = high.astype(BF)
+        for j in steps:
+            k = rem(a + j, na)
+            push(send_1.at[gh, k], recv_1.at[gh, a], sem_1.at[gh], along_a(k), 4)
+    for gh in range(halves):
+        arrived(recv_1.at[gh, pl.ds(0, na - 1)], sem_1.at[gh])
+        part = send_1[gh, a].astype(F32)
+        for j in range(1, na):
+            part = part + recv_1[gh, rem(a + j, na)].astype(F32)
+        for k in range(na):
+            send_2[gh, k] = part[:, k * width : (k + 1) * width].astype(BF)
+        for j in steps:
+            k = rem(b + j, na)
+            push(send_2.at[gh, k], recv_2.at[gh, b], sem_2.at[gh], along_b(k), 5)
     matched = rem(g + c, 2) == 0
     for gh in range(halves):
-        if gh % STEP == 0:
-            some = pl.ds(gh, min(STEP, halves - gh))
-            arrived(recv_1.at[pl.ds(0, places - 1), some], sem_1.at[gh])
-        part = recv_1[0, gh].astype(F32)
-        for k in range(1, places):
-            part = part + recv_1[k, gh].astype(F32)
+        arrived(recv_2.at[gh, pl.ds(0, na - 1)], sem_2.at[gh])
+        part = send_2[gh, b].astype(F32)
+        for j in range(1, na):
+            part = part + recv_2[gh, rem(b + j, na)].astype(F32)
         send_z[gh] = part.astype(BF)
         to = 2 * gh + c
         for zp in range(nzh):
@@ -499,7 +511,8 @@
     all_sent(0, buf_y.at[pl.ds(1, 2 * places - 1)])
     all_sent(2, buf_z.at[pl.ds(0, nz - 1)])
     all_sent(3, core_send)
-    all_sent(4, send_1.at[pl.ds(0, places - 1)])
+    all_sent(4, send_1.at[pl.ds(0, halves), pl.ds(0, na - 1)])
+    all_sent(5, send_2.at[pl.ds(0, halves), pl.ds(0, na - 1)])
     for cond, make in conditional:
 
         @pl.when(cond)
@@ -510,36 +523,17 @@
         copy.wait()
 
 
-def finish(na, count, *refs):
-    loss_hbm, pieces_hbm, squares_hbm, loss_out, g1_hbm, g2_hbm = refs[:6]
-    pieces, squares, g1_out, g2_out, sem = refs[6:]
-    into = [
-        pltpu.make_async_copy(pieces_hbm, pieces, sem.at[0]),
-        pltpu.make_async_copy(squares_hbm, squares, sem.at[1]),
-        pltpu.make_async_copy(loss_hbm, loss_out, sem.at[2]),
-    ]
-    for copy in into:
-        copy.start()
+def finish(na, count, loss_in, pieces, squares, loss_out, g1_out, g2_out):
     low = g2_out.shape[0] // na
     high = g1_out.shape[0] // na
     width = pieces.shape[2]
-    for copy in into[:2]:
-        copy.wait()
     factor = jnp.minimum(1.0, math.sqrt(count) / jnp.sqrt(squares[...] + 1e-06))
+    loss_out[...] = loss_in[...]
     for i in range(na):
         for k in range(na):
             column = slice(k * width, (k + 1) * width)
             g2_out[i * low : (i + 1) * low, column] = pieces[i * na + k, 0:low].astype(F32) * factor
             g1_out[i * high : (i + 1) * high, column] = pieces[i * na + k, low:].astype(F32) * factor
-    out = [
-        pltpu.make_async_copy(g1_out, g1_hbm, sem.at[3]),
-        pltpu.make_async_copy(g2_out, g2_hbm, sem.at[4]),
-    ]
-    for copy in out:
-        copy.start()
-    into[2].wait()
-    for copy in out:
-        copy.wait()
 
 
 def per_device(dims, features, w_first, w_second, table, heads, relations, tails, negatives, partner):
@@ -591,8 +585,10 @@
             V((d_hid, lanes), BF),
             V((halves, na, block, d_enc), BF),
             V((halves, na, block, d_enc), BF),
-            V((na * na, halves, block, width), BF),
-            V((na * na, halves, block, width), BF),
+            V((halves, na, block, d_enc), BF),
+            V((halves, na, block, d_enc), BF),
+            V((halves, na, block, width), BF),
+            V((halves, na, block, width), BF),
             V((halves, block, width), BF),
             V((nz, block, width), BF),
             V((na * na, 1, width), F32),
@@ -605,6 +601,7 @@
             S((1,)),
             S((nz,)),
             S((ng,)),
+            S((halves,)),
             S((halves,)),
             S((halves,)),
             S((1,)),
@@ -626,16 +623,8 @@
             jax.ShapeDtypeStruct((rows_1, d_hid), F32),
             jax.ShapeDtypeStruct((rows_2, d_enc), F32),
         ),
-        in_specs=[hbm] * 3,
-        out_specs=(vmem, hbm, hbm),
-        scratch_shapes=[
-            V((na * na, block, width), BF),
-            V((1, width), F32),
-            V((rows_1, d_hid), F32),
-            V((rows_2, d_enc), F32),
-            S((5,)),
-        ],
-        compiler_params=pltpu.CompilerParams(vmem_limit_bytes=60 * 1024 * 1024),
+        in_specs=[vmem] * 3,
+        out_specs=(vmem, vmem, vmem),
         name="finish",
     )(loss, pieces, squares)
 

time: 67.7 us -> 67.2 us (level)
  no operation moved by 1% of the time
where the time goes in v6:
time: 67.2 us; the launch traced here: 67 us
  Pallas kernels  66.3 us (99%)
    pallas_call x1, Pallas kernels, per_device(): pl.pallas_call(functools.partial(body, dims), out_shape=(jax.ShapeDtypeSt...  64.7 us
    pallas_call x1, Pallas kernels, per_device(): pl.pallas_call(functools.partial(finish, na, float(w_first.size + w_secon...  1.67 us

profile of v6, /device:TPU:1, one launch (start us, length us, event | category | flops | bytes accessed | tf_op | source)
XLA Modules:
  0.0 67.0 jit_solution(5394907805564460405)
XLA Ops:
  0.6 64.7 %step.1 = (f32[2,128]{1,0:T(2,128)}, bf16[16,40,128]{2,1,0:T(8,128)(2,1)}, f32[1,128]{1,0:T(1,128)}) custom-call(bf16[8,768]{1,0:T(8,128)(2,1)} %feat_hbm.1, bf16[768,512]{1,0:T(8,128)(2,1)} %w1_hbm.1, bf16[512,512]{1,0:T(8,128)(2,1)} %w2_hbm.1, bf16[1387,512]{1,0:T(8,128)(2,1)} %table_hbm.1, s32[2,128]{1,0:T(2,128)} %heads_hbm.1, s32[2,128]{1,0:T(2,128)} %rels_hbm.1, ...), custom_call_target="tpu_custom_call" | custom-call | tf_op jit(solution)/shard_map/step/pallas_call | solution.py:552
  65.3 1.7 %finish.1 = (f32[2,128]{1,0:T(2,128)}, f32[96,512]{1,0:T(8,128)}, f32[64,512]{1,0:T(8,128)}) custom-call(f32[2,128]{1,0:T(2,128)} %get-tuple-element.6.loss_in, bf16[16,40,128]{2,1,0:T(8,128)(2,1)} %get-tuple-element.7.pieces, f32[1,128]{1,0:T(1,128)} %get-tuple-element.8.squares), custom_call_target="tpu_custom_call" | custom-call | tf_op jit(solution)/shard_map/finish/pallas_call | solution.py:619

commit v7 on v5

--- a/solution.py
+++ b/solution.py
@@ -510,36 +510,17 @@
         copy.wait()
 
 
-def finish(na, count, *refs):
-    loss_hbm, pieces_hbm, squares_hbm, loss_out, g1_hbm, g2_hbm = refs[:6]
-    pieces, squares, g1_out, g2_out, sem = refs[6:]
-    into = [
-        pltpu.make_async_copy(pieces_hbm, pieces, sem.at[0]),
-        pltpu.make_async_copy(squares_hbm, squares, sem.at[1]),
-        pltpu.make_async_copy(loss_hbm, loss_out, sem.at[2]),
-    ]
-    for copy in into:
-        copy.start()
+def finish(na, count, loss_in, pieces, squares, loss_out, g1_out, g2_out):
     low = g2_out.shape[0] // na
     high = g1_out.shape[0] // na
     width = pieces.shape[2]
-    for copy in into[:2]:
-        copy.wait()
     factor = jnp.minimum(1.0, math.sqrt(count) / jnp.sqrt(squares[...] + 1e-06))
+    loss_out[...] = loss_in[...]
     for i in range(na):
         for k in range(na):
             column = slice(k * width, (k + 1) * width)
             g2_out[i * low : (i + 1) * low, column] = pieces[i * na + k, 0:low].astype(F32) * factor
             g1_out[i * high : (i + 1) * high, column] = pieces[i * na + k, low:].astype(F32) * factor
-    out = [
-        pltpu.make_async_copy(g1_out, g1_hbm, sem.at[3]),
-        pltpu.make_async_copy(g2_out, g2_hbm, sem.at[4]),
-    ]
-    for copy in out:
-        copy.start()
-    into[2].wait()
-    for copy in out:
-        copy.wait()
 
 
 def per_device(dims, features, w_first, w_second, table, heads, relations, tails, negatives, partner):
@@ -626,16 +607,8 @@
             jax.ShapeDtypeStruct((rows_1, d_hid), F32),
             jax.ShapeDtypeStruct((rows_2, d_enc), F32),
         ),
-        in_specs=[hbm] * 3,
-        out_specs=(vmem, hbm, hbm),
-        scratch_shapes=[
-            V((na * na, block, width), BF),
-            V((1, width), F32),
-            V((rows_1, d_hid), F32),
-            V((rows_2, d_enc), F32),
-            S((5,)),
-        ],
-        compiler_params=pltpu.CompilerParams(vmem_limit_bytes=60 * 1024 * 1024),
+        in_specs=[vmem] * 3,
+        out_specs=(vmem, vmem, vmem),
         name="finish",
     )(loss, pieces, squares)
 

time: 67.7 us -> 67.1 us (level)
  no operation moved by 1% of the time
where the time goes in v7:
time: 67.1 us; the launch traced here: 66.9 us
  Pallas kernels  66.2 us (99%)
    pallas_call x1, Pallas kernels, per_device(): pl.pallas_call(functools.partial(body, dims), out_shape=(jax.ShapeDtypeSt...  64.6 us
    pallas_call x1, Pallas kernels, per_device(): pl.pallas_call(functools.partial(finish, na, float(w_first.size + w_secon...  1.67 us

profile of v7, /device:TPU:1, one launch (start us, length us, event | category | flops | bytes accessed | tf_op | source)
XLA Modules:
  0.0 66.9 jit_solution(8805388602664908415)
XLA Ops:
  0.6 64.6 %step.1 = (f32[2,128]{1,0:T(2,128)}, bf16[16,40,128]{2,1,0:T(8,128)(2,1)}, f32[1,128]{1,0:T(1,128)}) custom-call(bf16[8,768]{1,0:T(8,128)(2,1)} %feat_hbm.1, bf16[768,512]{1,0:T(8,128)(2,1)} %w1_hbm.1, bf16[512,512]{1,0:T(8,128)(2,1)} %w2_hbm.1, bf16[1387,512]{1,0:T(8,128)(2,1)} %table_hbm.1, s32[2,128]{1,0:T(2,128)} %heads_hbm.1, s32[2,128]{1,0:T(2,128)} %rels_hbm.1, ...), custom_call_target="tpu_custom_call" | custom-call | tf_op jit(solution)/shard_map/step/pallas_call | solution.py:539
  65.2 1.7 %finish.1 = (f32[2,128]{1,0:T(2,128)}, f32[96,512]{1,0:T(8,128)}, f32[64,512]{1,0:T(8,128)}) custom-call(f32[2,128]{1,0:T(2,128)} %get-tuple-element.6.loss_in, bf16[16,40,128]{2,1,0:T(8,128)(2,1)} %get-tuple-element.7.pieces, f32[1,128]{1,0:T(1,128)} %get-tuple-element.8.squares), custom_call_target="tpu_custom_call" | custom-call | tf_op jit(solution)/shard_map/finish/pallas_call | solution.py:603
